TPU v7x, 32 devices: a whole 2x2x4 slice. The times are simulated.
32 devices in a mesh: tiles: 2 (over x), date: 8 (over z, y), row: 2 (over core).
Axes of the slice: x: 2, y: 2, z: 4, core: 2. Of those that a mesh axis runs over, the one named last changes fastest.
Arguments:
- slc_stack: bfloat16 [16, 2, 256, 1024], P('date', None, ('tiles', 'row')), parts along dimension 2, as said below
- partners: int32 [16, 4], P('date'), may hold values from 0 to 15, as said below
- counts: int32 [16], P('date'), may hold values from 1 to 4, as said below
- windows: int32 [16, 4], P('date'), may hold values from 3 to 5
Outputs:
- coherence: bfloat16 [16, 4, 256, 1024], P('date', None, ('tiles', 'row')), parts along dimension 2
There are 2 independent parts, one for each index of `tiles`. A program takes and returns all parts, laid end to end along the dimension named above; an argument that names none is the same for every part. Nothing has to cross between parts.
Inputs may be any that keep to these rules, and one draw needn't show every extreme that they name: The partners of date d are (d + o) mod 16 for distinct offsets o from 1 to 4; some date has a first partner exactly 4 ahead. `counts`: of the 2 dates held by one device along `date`, at most one has more than 2 pairs, so those dates have 6 pairs or fewer together; some device's pair of dates has exactly 6, and some date has 4. `slc_stack`: every pixel's magnitude is 0.5 or more.
All inputs are finite; a program needn't handle non-finite values.
Results may differ from a plain program's by a relative error of at most 0.001.
Values may be sent and summed in bfloat16 or wider, within the bound.
No kernel may reach another device: no remote copies, remote signals or barrier semaphores. Data moves between devices by JAX's collectives and lax.ppermute only.
A program may use at most 64 MiB of HBM per device.

v0:
```python
import jax
import jax.numpy as jnp
from jax import lax
from jax.sharding import PartitionSpec as P


def extended_2(shard, sides, width):
    for axis, dim in sides:
        count, length = (lax.axis_size(axis), shard.shape[dim])
        up = [(i, (i + 1) % count) for i in range(count - 1)]
        down = [(j, i) for i, j in up]
        last = lax.slice_in_dim(shard, length - width, length, axis=dim)
        leading = lax.slice_in_dim(shard, 0, width, axis=dim)
        before = lax.ppermute(last, axis, up)
        after = lax.ppermute(leading, axis, down)
        shard = jnp.concatenate([before, shard, after], axis=dim)
    return shard


def from_behind(shard, axis, by):
    count = lax.axis_size(axis)
    return lax.ppermute(shard, axis, [(i, (i + by) % count) for i in range(count)])


def pair_products(first_block, second_block):
    first_re = first_block[0].astype(jnp.float32)
    first_im = first_block[1].astype(jnp.float32)
    second_re = second_block[0].astype(jnp.float32)
    second_im = second_block[1].astype(jnp.float32)
    cross_re = first_re * second_re + first_im * second_im
    cross_im = first_im * second_re - first_re * second_im
    power_first = first_re * first_re + first_im * first_im
    power_second = second_re * second_re + second_im * second_im
    return jnp.stack([cross_re, cross_im, power_first, power_second])


def range_boxcar(stacked, half_width):
    columns = stacked.shape[-1]
    padded = jnp.pad(stacked, ((0, 0), (0, 0), (5, 5)))
    summed = jnp.zeros_like(stacked)
    for offset in range(-5, 6):
        weight = jnp.where(half_width >= abs(offset), 1.0, 0.0).astype(jnp.float32)
        summed = summed + weight * padded[:, :, 5 + offset : 5 + offset + columns]
    return summed


def row_boxcar(extended, strip_rows):
    summed = extended[:, 0:strip_rows, :]
    for offset in range(1, 5):
        summed = summed + extended[:, offset : offset + strip_rows, :]
    return summed


def coherence_of(sums):
    magnitude = jnp.sqrt(sums[0] * sums[0] + sums[1] * sums[1])
    return magnitude / jnp.sqrt(sums[2] * sums[3])


def pair_value(window, own_index, partner_date, half_width, first_date, total_dates, strip_rows):
    local_index = jnp.mod(partner_date - first_date, total_dates)
    first_block = lax.dynamic_index_in_dim(window, own_index, 0, keepdims=False)
    second_block = lax.dynamic_index_in_dim(window, local_index, 0, keepdims=False)
    summed = range_boxcar(pair_products(first_block, second_block), half_width)
    summed = extended_2(summed, (("row", 1),), 2)
    return coherence_of(row_boxcar(summed, strip_rows))


def run_items(
    window,
    first_date,
    total_dates,
    strip_rows,
    own_index,
    flat_partners,
    flat_widths,
    needed,
    capacity,
):
    item_total = own_index.shape[0]

    def compute(state_in, slot_item):
        index_own, partner_date, half_width, used_flag = slot_item
        result = pair_value(
            window, index_own, partner_date, half_width, first_date, total_dates, strip_rows
        )
        return (state_in, jnp.where(used_flag, result, 0.0).astype(jnp.bfloat16))

    item_ids = jnp.arange(item_total, dtype=jnp.int32)
    ranking = jnp.where(needed, 0, 1).astype(jnp.int32) * item_total + item_ids
    ordering = jnp.argsort(ranking, stable=True)[0:capacity]
    unused_state, values = lax.scan(
        compute,
        jnp.int32(0),
        (own_index[ordering], flat_partners[ordering], flat_widths[ordering], needed[ordering]),
    )
    blocks = jnp.zeros((item_total,) + values.shape[1:], jnp.bfloat16).at[ordering].set(values)
    return blocks


def local(slc_stack, partners, counts, windows):
    dates_dev = slc_stack.shape[0]
    strip_rows = slc_stack.shape[2]
    per_date = partners.shape[1]
    slot_total = dates_dev * per_date
    loop_size = lax.axis_size("date")
    reach_blocks = loop_size // 4
    total_dates = dates_dev * loop_size
    first_date = lax.axis_index("date") * dates_dev
    half_count = per_date // 2
    capacity = dates_dev * half_count + per_date - half_count
    slot_ids = jnp.arange(slot_total, dtype=jnp.int32)
    local_dates = slot_ids // per_date
    flat_partners = partners.reshape(slot_total)
    flat_widths = windows.reshape(slot_total)
    is_used = slot_ids % per_date < jnp.repeat(counts, per_date)
    pieces = [slc_stack]
    current = slc_stack
    for distance in range(reach_blocks):
        current = from_behind(current, "date", -1)
        pieces.append(current)
    window = jnp.concatenate(pieces, axis=0)
    blocks = run_items(
        window,
        first_date,
        total_dates,
        strip_rows,
        local_dates,
        flat_partners,
        flat_widths,
        is_used,
        capacity,
    )
    return blocks.reshape(dates_dev, per_date, strip_rows, slc_stack.shape[3])


def solution(mesh):
    in_specs = (
        P("date", None, ("tiles", "row"), None),
        P("date", None),
        P("date"),
        P("date", None),
    )
    out_specs = P("date", None, ("tiles", "row"), None)
    return jax.shard_map(local, mesh=mesh, in_specs=in_specs, out_specs=out_specs, check_vma=False)
```

profile of v0, /device:TPU:0, one launch (start us, length us, event | category | flops | bytes accessed | tf_op | source)
XLA Modules:
  0.0 148.8 jit_solution(11523229353198327064)
XLA Ops:
  0.0 6.0 %collective-permute-start.2 = (bf16[2,2,64,1024]{3,2,1,0:T(8,128)(2,1)}, bf16[2,2,64,1024]{3,2,1,0:T(8,128)(2,1)S(1)}, u32[]{:S(2)}, u32[]{:S(2)}) collective-permute-start(bf16[2,2,64,1024]{3,2,1,0:T(8,128)(2,1)} %param.6), channel_id=1, source_target_pairs={{0,14},{2,0},{4,2},{6,4},{8,6},{10,8},{12,10},{14,12},{1,15},{3,1}... | collective-permute-start | bytes 1572872 | tf_op jit(solution)/shard_map/ppermute | solution.py:22
  6.8 10.7 %collective-permute-done.2 = bf16[2,2,64,1024]{3,2,1,0:T(8,128)(2,1)S(1)} collective-permute-done((bf16[2,2,64,1024]{3,2,1,0:T(8,128)(2,1)}, bf16[2,2,64,1024]{3,2,1,0:T(8,128)(2,1)S(1)}, u32[]{:S(2)}, u32[]{:S(2)}) %collective-permute-start.2) | collective-permute-done | bytes 524320 | tf_op jit(solution)/shard_map/ppermute | solution.py:22
  17.5 5.1 %collective-permute-start.3 = (bf16[2,2,64,1024]{3,2,1,0:T(8,128)(2,1)S(1)}, bf16[2,2,64,1024]{3,2,1,0:T(8,128)(2,1)}, u32[]{:S(2)}, u32[]{:S(2)}) collective-permute-start(bf16[2,2,64,1024]{3,2,1,0:T(8,128)(2,1)S(1)} %collective-permute-done.2), channel_id=1, source_target_pairs={{0,14},{2,0},{4,2},{6,4},{8,6},{10,8},{12,10},{14,12},{1,15},{3,1}... | collective-permute-start | bytes 1572872 | tf_op jit(solution)/shard_map/ppermute | solution.py:22
  27.6 5.3 %collective-permute-done.3 = bf16[2,2,64,1024]{3,2,1,0:T(8,128)(2,1)} collective-permute-done((bf16[2,2,64,1024]{3,2,1,0:T(8,128)(2,1)S(1)}, bf16[2,2,64,1024]{3,2,1,0:T(8,128)(2,1)}, u32[]{:S(2)}, u32[]{:S(2)}) %collective-permute-start.3) | collective-permute-done | bytes 524320 | tf_op jit(solution)/shard_map/ppermute | solution.py:22
  34.2 112.7 %while.12 = (s32[]{:T(128)}, bf16[6,64,1024]{2,1,0:T(8,128)(2,1)S(1)}, pred[6]{0:T(512)(128)(4,1)S(1)}, s32[6]{0:T(128)S(1)}, s32[6]{0:T(128)S(1)}, /*index=5*/b...) while((s32[]{:T(128)}, ...), condition=%wide.region_2.3_spmd, body=%wide.region_1.2_spmd.sunk | while | flops 9895969 | bytes 9503421 | solution.py:91
  34.2 1.3 dynamic_slice.43
  43.7 2.8 %fusion.50 = f32[4,64,1024]{2,1,0:T(8,128)S(1)} fusion(f32[4,64,1024]{2,1,0:T(8,128)S(1)} %pad_maximum_fusion.5, f32[]{:T(128)} %bitcast.31, f32[]{:T(128)} %bitcast.32, f32[]{:T(128)} %bitcast.33, f32[]{:T(128)} %bitcast.34, f32[]{:T(128)} %bitcast.35, f32[]{:T(128)} %bitcast.36), kind=kLoop, calls=%fused_computation.29.clone.1 | loop fusion | flops 5505024 | bytes 2097176 | tf_op jit(solution)/shard_map/while/body/eval_jaxpr/add | solution.py:43
  46.5 1.3 collective-permute-start
  47.8 3.0 %collective-permute-start.1 = (f32[4,2,1024]{2,1,0:T(2,128)S(1)}, f32[4,2,1024]{2,1,0:T(2,128)S(1)}, u32[]{:S(2)}, u32[]{:S(2)}) collective-permute-start(f32[4,2,1024]{2,1,0:T(2,128)S(1)} %get-tuple-element.195), channel_id=1, source_target_pairs={{0,1},{2,3},{4,5},{6,7},{8,9},{10,11},{12,13},{14,15},{16,17},{18,... | collective-permute-start | bytes 98312 | tf_op jit(solution)/shard_map/while/body/eval_jaxpr/ppermute | solution.py:14
  62.5 2.8 %fusion.50 = f32[4,64,1024]{2,1,0:T(8,128)S(1)} fusion(f32[4,64,1024]{2,1,0:T(8,128)S(1)} %pad_maximum_fusion.5, f32[]{:T(128)} %bitcast.31, f32[]{:T(128)} %bitcast.32, f32[]{:T(128)} %bitcast.33, f32[]{:T(128)} %bitcast.34, f32[]{:T(128)} %bitcast.35, f32[]{:T(128)} %bitcast.36), kind=kLoop, calls=%fused_computation.29.clone.1 | loop fusion | flops 5505024 | bytes 2097176 | tf_op jit(solution)/shard_map/while/body/eval_jaxpr/add | solution.py:43
  65.3 1.3 collective-permute-start
  66.6 3.0 %collective-permute-start.1 = (f32[4,2,1024]{2,1,0:T(2,128)S(1)}, f32[4,2,1024]{2,1,0:T(2,128)S(1)}, u32[]{:S(2)}, u32[]{:S(2)}) collective-permute-start(f32[4,2,1024]{2,1,0:T(2,128)S(1)} %get-tuple-element.195), channel_id=1, source_target_pairs={{0,1},{2,3},{4,5},{6,7},{8,9},{10,11},{12,13},{14,15},{16,17},{18,... | collective-permute-start | bytes 98312 | tf_op jit(solution)/shard_map/while/body/eval_jaxpr/ppermute | solution.py:14
  81.3 2.8 %fusion.50 = f32[4,64,1024]{2,1,0:T(8,128)S(1)} fusion(f32[4,64,1024]{2,1,0:T(8,128)S(1)} %pad_maximum_fusion.5, f32[]{:T(128)} %bitcast.31, f32[]{:T(128)} %bitcast.32, f32[]{:T(128)} %bitcast.33, f32[]{:T(128)} %bitcast.34, f32[]{:T(128)} %bitcast.35, f32[]{:T(128)} %bitcast.36), kind=kLoop, calls=%fused_computation.29.clone.1 | loop fusion | flops 5505024 | bytes 2097176 | tf_op jit(solution)/shard_map/while/body/eval_jaxpr/add | solution.py:43
  84.1 1.3 collective-permute-start
  85.4 3.0 %collective-permute-start.1 = (f32[4,2,1024]{2,1,0:T(2,128)S(1)}, f32[4,2,1024]{2,1,0:T(2,128)S(1)}, u32[]{:S(2)}, u32[]{:S(2)}) collective-permute-start(f32[4,2,1024]{2,1,0:T(2,128)S(1)} %get-tuple-element.195), channel_id=1, source_target_pairs={{0,1},{2,3},{4,5},{6,7},{8,9},{10,11},{12,13},{14,15},{16,17},{18,... | collective-permute-start | bytes 98312 | tf_op jit(solution)/shard_map/while/body/eval_jaxpr/ppermute | solution.py:14
  100.1 2.8 %fusion.50 = f32[4,64,1024]{2,1,0:T(8,128)S(1)} fusion(f32[4,64,1024]{2,1,0:T(8,128)S(1)} %pad_maximum_fusion.5, f32[]{:T(128)} %bitcast.31, f32[]{:T(128)} %bitcast.32, f32[]{:T(128)} %bitcast.33, f32[]{:T(128)} %bitcast.34, f32[]{:T(128)} %bitcast.35, f32[]{:T(128)} %bitcast.36), kind=kLoop, calls=%fused_computation.29.clone.1 | loop fusion | flops 5505024 | bytes 2097176 | tf_op jit(solution)/shard_map/while/body/eval_jaxpr/add | solution.py:43
  102.9 1.3 collective-permute-start
  104.2 3.0 %collective-permute-start.1 = (f32[4,2,1024]{2,1,0:T(2,128)S(1)}, f32[4,2,1024]{2,1,0:T(2,128)S(1)}, u32[]{:S(2)}, u32[]{:S(2)}) collective-permute-start(f32[4,2,1024]{2,1,0:T(2,128)S(1)} %get-tuple-element.195), channel_id=1, source_target_pairs={{0,1},{2,3},{4,5},{6,7},{8,9},{10,11},{12,13},{14,15},{16,17},{18,... | collective-permute-start | bytes 98312 | tf_op jit(solution)/shard_map/while/body/eval_jaxpr/ppermute | solution.py:14
  118.9 2.8 %fusion.50 = f32[4,64,1024]{2,1,0:T(8,128)S(1)} fusion(f32[4,64,1024]{2,1,0:T(8,128)S(1)} %pad_maximum_fusion.5, f32[]{:T(128)} %bitcast.31, f32[]{:T(128)} %bitcast.32, f32[]{:T(128)} %bitcast.33, f32[]{:T(128)} %bitcast.34, f32[]{:T(128)} %bitcast.35, f32[]{:T(128)} %bitcast.36), kind=kLoop, calls=%fused_computation.29.clone.1 | loop fusion | flops 5505024 | bytes 2097176 | tf_op jit(solution)/shard_map/while/body/eval_jaxpr/add | solution.py:43
  121.7 1.3 collective-permute-start
  123.0 3.0 %collective-permute-start.1 = (f32[4,2,1024]{2,1,0:T(2,128)S(1)}, f32[4,2,1024]{2,1,0:T(2,128)S(1)}, u32[]{:S(2)}, u32[]{:S(2)}) collective-permute-start(f32[4,2,1024]{2,1,0:T(2,128)S(1)} %get-tuple-element.195), channel_id=1, source_target_pairs={{0,1},{2,3},{4,5},{6,7},{8,9},{10,11},{12,13},{14,15},{16,17},{18,... | collective-permute-start | bytes 98312 | tf_op jit(solution)/shard_map/while/body/eval_jaxpr/ppermute | solution.py:14
  137.7 2.8 %fusion.50 = f32[4,64,1024]{2,1,0:T(8,128)S(1)} fusion(f32[4,64,1024]{2,1,0:T(8,128)S(1)} %pad_maximum_fusion.5, f32[]{:T(128)} %bitcast.31, f32[]{:T(128)} %bitcast.32, f32[]{:T(128)} %bitcast.33, f32[]{:T(128)} %bitcast.34, f32[]{:T(128)} %bitcast.35, f32[]{:T(128)} %bitcast.36), kind=kLoop, calls=%fused_computation.29.clone.1 | loop fusion | flops 5505024 | bytes 2097176 | tf_op jit(solution)/shard_map/while/body/eval_jaxpr/add | solution.py:43
  140.5 1.3 collective-permute-start
  141.8 3.0 %collective-permute-start.1 = (f32[4,2,1024]{2,1,0:T(2,128)S(1)}, f32[4,2,1024]{2,1,0:T(2,128)S(1)}, u32[]{:S(2)}, u32[]{:S(2)}) collective-permute-start(f32[4,2,1024]{2,1,0:T(2,128)S(1)} %get-tuple-element.195), channel_id=1, source_target_pairs={{0,1},{2,3},{4,5},{6,7},{8,9},{10,11},{12,13},{14,15},{16,17},{18,... | collective-permute-start | bytes 98312 | tf_op jit(solution)/shard_map/while/body/eval_jaxpr/ppermute | solution.py:14
  (89 shorter events, 36.7 us)
Async XLA Ops:
  0.0 32.9 %copy-start.1 = (bf16[2,2,64,1024]{3,2,1,0:T(8,128)(2,1)S(1)}, bf16[2,2,64,1024]{3,2,1,0:T(8,128)(2,1)}, u32[]{:S(2)}) copy-start(bf16[2,2,64,1024]{3,2,1,0:T(8,128)(2,1)} %param.6) | copy-start | bytes 1572868
  0.0 26.3 %copy-start.2 = (s32[2,4]{1,0:T(2,128)S(1)}, s32[2,4]{1,0:T(2,128)}, u32[]{:S(2)}) copy-start(s32[2,4]{1,0:T(2,128)} %param.7) | copy-start | bytes 100
  0.0 17.5 %collective-permute-start.2 = (bf16[2,2,64,1024]{3,2,1,0:T(8,128)(2,1)}, bf16[2,2,64,1024]{3,2,1,0:T(8,128)(2,1)S(1)}, u32[]{:S(2)}, u32[]{:S(2)}) collective-permute-start(bf16[2,2,64,1024]{3,2,1,0:T(8,128)(2,1)} %param.6), channel_id=1, source_target_pairs={{0,14},{2,0},{4,2},{6,4},{8,6},{10,8},{12,10},{14,12},{1,15},{3,1}... | collective-permute-start | bytes 1572872 | tf_op jit(solution)/shard_map/ppermute | solution.py:22
  17.5 15.4 %collective-permute-start.3 = (bf16[2,2,64,1024]{3,2,1,0:T(8,128)(2,1)S(1)}, bf16[2,2,64,1024]{3,2,1,0:T(8,128)(2,1)}, u32[]{:S(2)}, u32[]{:S(2)}) collective-permute-start(bf16[2,2,64,1024]{3,2,1,0:T(8,128)(2,1)S(1)} %collective-permute-done.2), channel_id=1, source_target_pairs={{0,14},{2,0},{4,2},{6,4},{8,6},{10,8},{12,10},{14,12},{1,15},{3,1}... | collective-permute-start | bytes 1572872 | tf_op jit(solution)/shard_map/ppermute | solution.py:22
  46.5 5.0 %collective-permute-start = (f32[4,2,1024]{2,1,0:T(2,128)S(1)}, f32[4,2,1024]{2,1,0:T(2,128)S(1)}, u32[]{:S(2)}, u32[]{:S(2)}) collective-permute-start(f32[4,2,1024]{2,1,0:T(2,128)S(1)} %get-tuple-element.194), channel_id=1, source_target_pairs={{1,0},{3,2},{5,4},{7,6},{9,8},{11,10},{13,12},{15,14},{17,16},{19,... | collective-permute-start | bytes 98312 | tf_op jit(solution)/shard_map/while/body/eval_jaxpr/ppermute | solution.py:15
  47.8 3.9 %collective-permute-start.1 = (f32[4,2,1024]{2,1,0:T(2,128)S(1)}, f32[4,2,1024]{2,1,0:T(2,128)S(1)}, u32[]{:S(2)}, u32[]{:S(2)}) collective-permute-start(f32[4,2,1024]{2,1,0:T(2,128)S(1)} %get-tuple-element.195), channel_id=1, source_target_pairs={{0,1},{2,3},{4,5},{6,7},{8,9},{10,11},{12,13},{14,15},{16,17},{18,... | collective-permute-start | bytes 98312 | tf_op jit(solution)/shard_map/while/body/eval_jaxpr/ppermute | solution.py:14
  65.3 5.0 %collective-permute-start = (f32[4,2,1024]{2,1,0:T(2,128)S(1)}, f32[4,2,1024]{2,1,0:T(2,128)S(1)}, u32[]{:S(2)}, u32[]{:S(2)}) collective-permute-start(f32[4,2,1024]{2,1,0:T(2,128)S(1)} %get-tuple-element.194), channel_id=1, source_target_pairs={{1,0},{3,2},{5,4},{7,6},{9,8},{11,10},{13,12},{15,14},{17,16},{19,... | collective-permute-start | bytes 98312 | tf_op jit(solution)/shard_map/while/body/eval_jaxpr/ppermute | solution.py:15
  66.6 3.9 %collective-permute-start.1 = (f32[4,2,1024]{2,1,0:T(2,128)S(1)}, f32[4,2,1024]{2,1,0:T(2,128)S(1)}, u32[]{:S(2)}, u32[]{:S(2)}) collective-permute-start(f32[4,2,1024]{2,1,0:T(2,128)S(1)} %get-tuple-element.195), channel_id=1, source_target_pairs={{0,1},{2,3},{4,5},{6,7},{8,9},{10,11},{12,13},{14,15},{16,17},{18,... | collective-permute-start | bytes 98312 | tf_op jit(solution)/shard_map/while/body/eval_jaxpr/ppermute | solution.py:14
  84.1 5.0 %collective-permute-start = (f32[4,2,1024]{2,1,0:T(2,128)S(1)}, f32[4,2,1024]{2,1,0:T(2,128)S(1)}, u32[]{:S(2)}, u32[]{:S(2)}) collective-permute-start(f32[4,2,1024]{2,1,0:T(2,128)S(1)} %get-tuple-element.194), channel_id=1, source_target_pairs={{1,0},{3,2},{5,4},{7,6},{9,8},{11,10},{13,12},{15,14},{17,16},{19,... | collective-permute-start | bytes 98312 | tf_op jit(solution)/shard_map/while/body/eval_jaxpr/ppermute | solution.py:15
  85.4 3.9 %collective-permute-start.1 = (f32[4,2,1024]{2,1,0:T(2,128)S(1)}, f32[4,2,1024]{2,1,0:T(2,128)S(1)}, u32[]{:S(2)}, u32[]{:S(2)}) collective-permute-start(f32[4,2,1024]{2,1,0:T(2,128)S(1)} %get-tuple-element.195), channel_id=1, source_target_pairs={{0,1},{2,3},{4,5},{6,7},{8,9},{10,11},{12,13},{14,15},{16,17},{18,... | collective-permute-start | bytes 98312 | tf_op jit(solution)/shard_map/while/body/eval_jaxpr/ppermute | solution.py:14
  102.9 5.0 %collective-permute-start = (f32[4,2,1024]{2,1,0:T(2,128)S(1)}, f32[4,2,1024]{2,1,0:T(2,128)S(1)}, u32[]{:S(2)}, u32[]{:S(2)}) collective-permute-start(f32[4,2,1024]{2,1,0:T(2,128)S(1)} %get-tuple-element.194), channel_id=1, source_target_pairs={{1,0},{3,2},{5,4},{7,6},{9,8},{11,10},{13,12},{15,14},{17,16},{19,... | collective-permute-start | bytes 98312 | tf_op jit(solution)/shard_map/while/body/eval_jaxpr/ppermute | solution.py:15
  104.2 3.9 %collective-permute-start.1 = (f32[4,2,1024]{2,1,0:T(2,128)S(1)}, f32[4,2,1024]{2,1,0:T(2,128)S(1)}, u32[]{:S(2)}, u32[]{:S(2)}) collective-permute-start(f32[4,2,1024]{2,1,0:T(2,128)S(1)} %get-tuple-element.195), channel_id=1, source_target_pairs={{0,1},{2,3},{4,5},{6,7},{8,9},{10,11},{12,13},{14,15},{16,17},{18,... | collective-permute-start | bytes 98312 | tf_op jit(solution)/shard_map/while/body/eval_jaxpr/ppermute | solution.py:14
  121.7 5.0 %collective-permute-start = (f32[4,2,1024]{2,1,0:T(2,128)S(1)}, f32[4,2,1024]{2,1,0:T(2,128)S(1)}, u32[]{:S(2)}, u32[]{:S(2)}) collective-permute-start(f32[4,2,1024]{2,1,0:T(2,128)S(1)} %get-tuple-element.194), channel_id=1, source_target_pairs={{1,0},{3,2},{5,4},{7,6},{9,8},{11,10},{13,12},{15,14},{17,16},{19,... | collective-permute-start | bytes 98312 | tf_op jit(solution)/shard_map/while/body/eval_jaxpr/ppermute | solution.py:15
  123.0 3.9 %collective-permute-start.1 = (f32[4,2,1024]{2,1,0:T(2,128)S(1)}, f32[4,2,1024]{2,1,0:T(2,128)S(1)}, u32[]{:S(2)}, u32[]{:S(2)}) collective-permute-start(f32[4,2,1024]{2,1,0:T(2,128)S(1)} %get-tuple-element.195), channel_id=1, source_target_pairs={{0,1},{2,3},{4,5},{6,7},{8,9},{10,11},{12,13},{14,15},{16,17},{18,... | collective-permute-start | bytes 98312 | tf_op jit(solution)/shard_map/while/body/eval_jaxpr/ppermute | solution.py:14
  140.5 5.0 %collective-permute-start = (f32[4,2,1024]{2,1,0:T(2,128)S(1)}, f32[4,2,1024]{2,1,0:T(2,128)S(1)}, u32[]{:S(2)}, u32[]{:S(2)}) collective-permute-start(f32[4,2,1024]{2,1,0:T(2,128)S(1)} %get-tuple-element.194), channel_id=1, source_target_pairs={{1,0},{3,2},{5,4},{7,6},{9,8},{11,10},{13,12},{15,14},{17,16},{19,... | collective-permute-start | bytes 98312 | tf_op jit(solution)/shard_map/while/body/eval_jaxpr/ppermute | solution.py:15
  141.8 3.9 %collective-permute-start.1 = (f32[4,2,1024]{2,1,0:T(2,128)S(1)}, f32[4,2,1024]{2,1,0:T(2,128)S(1)}, u32[]{:S(2)}, u32[]{:S(2)}) collective-permute-start(f32[4,2,1024]{2,1,0:T(2,128)S(1)} %get-tuple-element.195), channel_id=1, source_target_pairs={{0,1},{2,3},{4,5},{6,7},{8,9},{10,11},{12,13},{14,15},{16,17},{18,... | collective-permute-start | bytes 98312 | tf_op jit(solution)/shard_map/while/body/eval_jaxpr/ppermute | solution.py:14
  147.8 1.0 copy-start
where the time goes:
time: 150 us; the launch traced here: 149 us
  loops' own time  41.1 us (27%)
  starting transfers between devices  37 us (25%)
  other arithmetic  27.6 us (18%)
  local copies, waits for them, and re-layouts  25.7 us (17%)
  waiting for transfers between devices  17.3 us (12%)
    another operation x1, loops' own time, run_items(): lax.scan(compute, jnp.int32(0), (own_index[ordering], flat_partners[order...  41.1 us
    dynamic_slice x24, local copies, waits for them, and re-layouts, run_items(): lax.scan(compute, jnp.int32(0), (own_index[ordering], flat_partners[order...  18.8 us
    ppermute x6, starting transfers between devices, extended_2(): before = lax.ppermute(last, axis, up)  18.2 us
    add x6, other arithmetic, range_boxcar(): summed = summed + weight * padded[:, :, 5 + offset:5 + offset + columns]  16.6 us
    ppermute x2, waiting for transfers between devices, from_behind(): lax.ppermute(shard, axis, [(i, (i + by) % count) for i in range(count)])  16 us
    ppermute x2, starting transfers between devices, from_behind(): lax.ppermute(shard, axis, [(i, (i + by) % count) for i in range(count)])  11.1 us
    ppermute x6, starting transfers between devices, extended_2(): after = lax.ppermute(leading, axis, down)  7.75 us
    dynamic_update_slice x6, other arithmetic, run_items(): lax.scan(compute, jnp.int32(0), (own_index[ordering], flat_partners[order...  4.6 us
  transfers between devices with their start and end apart: 14, of which 8 were waited for; matrix products, arithmetic and copies ran while one was open for 6% of the time, Pallas kernels for 0%

commit v1 on v0

v1 whole, which is shorter than its diff:
```python
import functools

import jax
import jax.numpy as jnp
from jax import lax
from jax.experimental import pallas as pl
from jax.experimental.pallas import tpu as pltpu
from jax.sharding import PartitionSpec as P

REACH_COLS = 5
HALO = 2
LANES = 128
TOP = 8
SMALLEST = 1.1754944e-38


def stage_kernel(
    first_local,
    fill,
    total_dates,
    partners,
    counts,
    windows,
    own,
    own_edge,
    other,
    other_edge,
    previous,
    out,
    products,
    split,
    band,
    results,
    zeros,
    sems,
):
    del previous
    dates_dev, _, rows, cols = own.shape
    here = other.shape[0]
    per_date = partners.shape[1]
    slots = dates_dev * per_date
    stripes = cols // LANES
    first_date = lax.axis_index("date") * dates_dev
    upper = lax.axis_index("row") == 0

    def state(slot):
        date, place = slot // per_date, slot % per_date
        ahead = lax.rem(partners[date, place] - first_date + total_dates, total_dates) - first_local
        used = place < counts[date]
        mine = jnp.logical_and(used, jnp.logical_and(ahead >= 0, ahead < here))
        return date, place, jnp.clip(ahead, 0, here - 1), used, mine

    def copy_of(slot, source):
        return pltpu.make_async_copy(source, out.at[slot // per_date, slot % per_date], sems.at[slot])

    split[:, 0:LANES] = jnp.zeros((split.shape[0], LANES), jnp.bfloat16)
    split[:, LANES + cols :] = jnp.zeros((split.shape[0], LANES), jnp.bfloat16)
    if fill:
        zeros[...] = jnp.zeros_like(zeros)

        def clear(slot, carry):
            _, _, _, used, _ = state(slot)

            @pl.when(jnp.logical_not(used))
            def _():
                copy_of(slot, zeros).start()

            return carry

        lax.fori_loop(0, slots, clear, 0)

    def planes(first_re, first_im, second_re, second_im):
        first_re, first_im = first_re.astype(jnp.float32), first_im.astype(jnp.float32)
        second_re, second_im = second_re.astype(jnp.float32), second_im.astype(jnp.float32)
        return (
            first_re * second_re + first_im * second_im,
            first_im * second_re - first_re * second_im,
            first_re * first_re + first_im * first_im,
            second_re * second_re + second_im * second_im,
        )

    def one_slot(slot, carry):
        date, place, ahead, _, mine = state(slot)

        @pl.when(mine)
        def _():
            half_width = windows[date, place]
            depth = lax.broadcasted_iota(jnp.int32, band.shape, 0)
            width = lax.broadcasted_iota(jnp.int32, band.shape, 1)
            band[...] = jnp.where(jnp.abs(depth - LANES - width) <= half_width, 1.0, 0.0).astype(jnp.bfloat16)
            for stripe in range(stripes):
                at = slice(stripe * LANES, (stripe + 1) * LANES)
                main = planes(own[date, 0, :, at], own[date, 1, :, at], other[ahead, 0, :, at], other[ahead, 1, :, at])
                edge = planes(
                    own_edge[date, 0, :, at], own_edge[date, 1, :, at], other_edge[ahead, 0, :, at], other_edge[ahead, 1, :, at]
                )
                for k in range(4):
                    products[k, TOP : TOP + rows, :] = main[k]
                    products[k, TOP - HALO : TOP, :] = jnp.where(upper, 0.0, edge[k])
                    products[k, TOP + rows : TOP + rows + HALO, :] = jnp.where(upper, edge[k], 0.0)
                for k in range(4):
                    total = products[k, TOP - HALO : TOP - HALO + rows, :]
                    for shift in range(1, 2 * HALO + 1):
                        total = total + products[k, TOP - HALO + shift : TOP - HALO + shift + rows, :]
                    high = total.astype(jnp.bfloat16)
                    low = (total - high.astype(jnp.float32)).astype(jnp.bfloat16)
                    into = slice(LANES + stripe * LANES, LANES + (stripe + 1) * LANES)
                    split[k * 2 * rows : k * 2 * rows + rows, into] = high
                    split[k * 2 * rows + rows : (k + 1) * 2 * rows, into] = low
            block = band.shape[1]
            for j in range(cols // block):
                box = jnp.dot(
                    split[:, j * block : j * block + band.shape[0]], band[...], preferred_element_type=jnp.float32
                )
                sums = [box[k * 2 * rows : k * 2 * rows + rows] + box[k * 2 * rows + rows : (k + 1) * 2 * rows] for k in range(4)]
                square = sums[0] * sums[0] + sums[1] * sums[1]
                magnitude = square * lax.rsqrt(jnp.maximum(square, SMALLEST))
                value = magnitude * lax.rsqrt(sums[2] * sums[3])
                results[slot, :, j * block : (j + 1) * block] = value.astype(jnp.bfloat16)
            copy_of(slot, results.at[slot]).start()

        return carry

    lax.fori_loop(0, slots, one_slot, 0)

    def finish(slot, carry):
        _, _, _, used, mine = state(slot)
        started = jnp.logical_or(mine, jnp.logical_not(used)) if fill else mine

        @pl.when(started)
        def _():
            copy_of(slot, results.at[slot]).wait()

        return carry

    lax.fori_loop(0, slots, finish, 0)


def stage(first_local, total_dates, tables, own, own_edge, other, other_edge, previous):
    dates_dev, _, rows, cols = own.shape
    per_date = tables[0].shape[1]
    slots = dates_dev * per_date
    shape = jax.ShapeDtypeStruct((dates_dev, per_date, rows, cols), jnp.bfloat16)
    fill = previous is None
    kernel = functools.partial(stage_kernel, first_local, fill, total_dates)
    if fill:
        inner = kernel

        def kernel(*refs):
            inner(*refs[:7], None, *refs[7:])

    smem = pl.BlockSpec(memory_space=pltpu.SMEM)
    vmem = pl.BlockSpec(memory_space=pltpu.VMEM)
    anywhere = pl.BlockSpec(memory_space=pl.ANY)
    block = 2 * LANES
    return pl.pallas_call(
        kernel,
        out_shape=shape,
        in_specs=[smem] * 3 + [vmem] * 4 + ([] if fill else [anywhere]),
        out_specs=anywhere,
        scratch_shapes=[
            pltpu.VMEM((4, rows + 2 * TOP, LANES), jnp.float32),
            pltpu.VMEM((8 * rows, cols + 2 * LANES), jnp.bfloat16),
            pltpu.VMEM((2 * block, block), jnp.bfloat16),
            pltpu.VMEM((slots, rows, cols), jnp.bfloat16),
            pltpu.VMEM((rows, cols), jnp.bfloat16),
            pltpu.SemaphoreType.DMA((slots,)),
        ],
        input_output_aliases={} if fill else {7: 0},
        name=f"stage_{first_local}",
        cost_estimate=pl.CostEstimate(flops=1 << 30, bytes_accessed=1 << 22, transcendentals=0),
    )(*tables, own, own_edge, other, other_edge, *([] if fill else [previous]))


def local(slc_stack, partners, counts, windows):
    dates_dev, _, rows, _ = slc_stack.shape
    loop_size = lax.axis_size("date")
    strips = lax.axis_size("row")
    assert strips == 2
    reach = loop_size // 4
    total_dates = dates_dev * loop_size
    tables = (partners, counts, windows)
    edge = jnp.where(lax.axis_index("row") == 0, slc_stack[:, :, rows - HALO :], slc_stack[:, :, :HALO])
    blocks = []
    for distance in range(1, reach + 1):
        blocks.append(lax.ppermute(slc_stack, "date", [((i + distance) % loop_size, i) for i in range(loop_size)]))
    edges = []
    for distance in range(reach + 1):
        pairs = [
            (((i + distance) % loop_size) * strips + (1 - r), i * strips + r) for i in range(loop_size) for r in range(strips)
        ]
        edges.append(lax.ppermute(edge, ("date", "row"), pairs))
    out = stage(0, total_dates, tables, slc_stack, edges[0], slc_stack, edges[0], None)
    for distance in range(1, reach + 1):
        out = stage(
            distance * dates_dev, total_dates, tables, slc_stack, edges[0], blocks[distance - 1], edges[distance], out
        )
    return out


def solution(mesh):
    in_specs = (
        P("date", None, ("tiles", "row"), None),
        P("date", None),
        P("date"),
        P("date", None),
    )
    out_specs = P("date", None, ("tiles", "row"), None)
    return jax.shard_map(local, mesh=mesh, in_specs=in_specs, out_specs=out_specs, check_vma=False)
```

time: 150 us -> 39.7 us (0.26)
  loops' own time: 41.1 us -> 0 us
  starting transfers between devices: 37 us -> 7.28 us
  other arithmetic: 27.6 us -> 0.9 us
  local copies, waits for them, and re-layouts: 25.7 us -> 3.38 us
  Pallas kernels: 0 us -> 9.68 us
    another operation x1 -> x0, loops' own time: 41.1 us -> none  [run_items(): lax.scan(compute, jnp.int32(0), (own_index[ordering], flat_partners[order...]
    ppermute x14 -> x5, starting transfers between devices: 37 us -> 7.28 us  [the longest x2 6.48 us: local(): lax.ppermute(slc_stack, 'date', [((i + distance) % loop_size, i) for i in...]
    add x19 -> x0, other arithmetic: 20.4 us -> none  [the longest x6 16.6 us: range_boxcar(): summed = summed + weight * padded[:, :, 5 + offset:5 + offset + columns]]
    dynamic_slice x24 -> x0, local copies, waits for them, and re-layouts: 18.8 us -> none  [run_items(): lax.scan(compute, jnp.int32(0), (own_index[ordering], flat_partners[order...]
    pallas_call x0 -> x3, Pallas kernels: none -> 9.68 us  [stage(): pl.pallas_call(kernel, out_shape=shape, in_specs=[smem] * 3 + [vmem] * 4...]
    dynamic_update_slice x6 -> x0, other arithmetic: 4.6 us -> none  [run_items(): lax.scan(compute, jnp.int32(0), (own_index[ordering], flat_partners[order...]
    gather x4 -> x0, local copies, waits for them, and re-layouts: 3.16 us -> none  [the longest x1 1.22 us: run_items(): flat_partners[ordering]]
    unnamed x6 -> x10, local copies, waits for them, and re-layouts: 0.97 us -> 3.38 us
  transfers between devices with their start and end apart: 14 -> 5, of which waited for: 8 -> 2; matrix products, arithmetic and copies ran while one was open for 6% -> 2% of each run, Pallas kernels for 0% -> 14%
where the time goes in v1:
time: 39.7 us; the launch traced here: 39.4 us
  waiting for transfers between devices  18.1 us (46%)
  Pallas kernels  9.68 us (24%)
  starting transfers between devices  7.28 us (18%)
  local copies, waits for them, and re-layouts  3.38 us (9%)
  other arithmetic  0.9 us (2%)
    ppermute x3, waiting for transfers between devices, local(): edges.append(lax.ppermute(edge, ('date', 'row'), pairs))  18.1 us
    pallas_call x3, Pallas kernels, stage(): pl.pallas_call(kernel, out_shape=shape, in_specs=[smem] * 3 + [vmem] * 4...  9.68 us
    ppermute x2, starting transfers between devices, local(): lax.ppermute(slc_stack, 'date', [((i + distance) % loop_size, i) for i in...  6.48 us
    unnamed x10, local copies, waits for them, and re-layouts  3.38 us
    select_n x1, other arithmetic, local(): jnp.where(lax.axis_index('row') == 0, slc_stack[:, :, rows - HALO:], slc_...  0.9 us
    ppermute x3, starting transfers between devices, local(): edges.append(lax.ppermute(edge, ('date', 'row'), pairs))  0.8 us
  transfers between devices with their start and end apart: 5, of which 2 were waited for; matrix products, arithmetic and copies ran while one was open for 2% of the time, Pallas kernels for 14%

profile of v1, /device:TPU:0, one launch (start us, length us, event | category | flops | bytes accessed | tf_op | source)
XLA Modules:
  0.0 39.4 jit_solution(15823545793845872489)
XLA Ops:
  0.0 6.0 %collective-permute-start.3 = (bf16[2,2,64,1024]{3,2,1,0:T(8,128)(2,1)}, bf16[2,2,64,1024]{3,2,1,0:T(8,128)(2,1)S(1)}, u32[]{:S(2)}, u32[]{:S(2)}) collective-permute-start(bf16[2,2,64,1024]{3,2,1,0:T(8,128)(2,1)} %own.3), channel_id=1, source_target_pairs={{2,0},{4,2},{6,4},{8,6},{10,8},{12,10},{14,12},{0,14},{3,1},{5,3},... | collective-permute-start | bytes 1572872 | tf_op jit(solution)/shard_map/ppermute | solution.py:186
  6.0 0.4 %collective-permute-start.1 = (bf16[2,2,64,1024]{3,2,1,0:T(8,128)(2,1)}, bf16[2,2,64,1024]{3,2,1,0:T(8,128)(2,1)S(1)}, u32[]{:S(2)}, u32[]{:S(2)}) collective-permute-start(bf16[2,2,64,1024]{3,2,1,0:T(8,128)(2,1)} %own.3), channel_id=1, source_target_pairs={{4,0},{6,2},{8,4},{10,6},{12,8},{14,10},{0,12},{2,14},{5,1},{7,3},... | collective-permute-start | bytes 1572872 | tf_op jit(solution)/shard_map/ppermute | solution.py:186
  6.5 0.9 %broadcast_select_fusion = bf16[2,2,2,1024]{3,2,1,0:T(2,128)(2,1)S(1)} fusion(pred[]{:T(512)S(6)} %eq.3, bf16[2,2,64,1024]{3,2,1,0:T(8,128)(2,1)} %own.3), kind=kLoop, calls=%fused_computation | loop fusion | flops 8192 | bytes 49153 | tf_op jit(solution)/shard_map/jit(_where)/select_n | solution.py:183
  7.4 0.1 collective-permute-start
  7.5 0.6 %collective-permute-start.4 = (bf16[2,2,2,1024]{3,2,1,0:T(2,128)(2,1)S(1)}, bf16[2,2,2,1024]{3,2,1,0:T(2,128)(2,1)S(1)}, u32[]{:S(2)}, u32[]{:S(2)}) collective-permute-start(bf16[2,2,2,1024]{3,2,1,0:T(2,128)(2,1)S(1)} %broadcast_select_fusion), channel_id=1, source_target_pairs={{3,0},{2,1},{5,2},{4,3},{7,4},{6,5},{9,6},{8,7},{11,8},{10,9},{13,... | collective-permute-start | bytes 49160 | tf_op jit(solution)/shard_map/ppermute | solution.py:192
  8.1 0.1 collective-permute-start.2
  8.2 0.4 %collective-permute-done.refs_4_.refs_6_.own_edge = bf16[2,2,2,1024]{3,2,1,0:T(2,128)(2,1)S(1)} collective-permute-done((bf16[2,2,2,1024]{3,2,1,0:T(2,128)(2,1)S(1)}, bf16[2,2,2,1024]{3,2,1,0:T(2,128)(2,1)S(1)}, u32[]{:S(2)}, u32[]{:S(2)}) %collective-permute-start) | collective-permute-done | bytes 16416 | tf_op jit(solution)/shard_map/ppermute | solution.py:192
  8.6 0.0 copy-start.2
  8.6 0.6 %copy-done.2 = bf16[2,2,2,1024]{3,2,1,0:T(2,128)(2,1)} copy-done((bf16[2,2,2,1024]{3,2,1,0:T(2,128)(2,1)}, bf16[2,2,2,1024]{3,2,1,0:T(2,128)(2,1)S(1)}, u32[]{:S(2)}) %copy-start.2) | copy-done | bytes 16408
  9.2 2.3 %stage_0.1.previous = bf16[2,4,64,1024]{3,2,1,0:T(8,128)(2,1)} custom-call(s32[2,4]{1,0:T(2,128)} %partners.3, s32[2]{0:T(128)} %counts.3, s32[2,4]{1,0:T(2,128)} %windows.3, bf16[2,2,64,1024]{3,2,1,0:T(8,128)(2,1)} %own.3, bf16[2,2,2,1024]{3,2,1,0:T(2,128)(2,1)} %copy-done.2, bf16[2,2,64,1024]{3,2,1,0:T(8,128)(2,1)} %own.3, bf16[2,2,2,1024]{3,2,1,0:T(2,128)(2,1)} %copy-done.2), custom_call_target="tpu_custom_call" | custom-call | flops 1073741824 | bytes 4194304 | tf_op jit(solution)/shard_map/stage_0/pallas_call | solution.py:156
  11.5 17.7 %collective-permute-done.4.other_edge = bf16[2,2,2,1024]{3,2,1,0:T(2,128)(2,1)S(1)} collective-permute-done((bf16[2,2,2,1024]{3,2,1,0:T(2,128)(2,1)S(1)}, bf16[2,2,2,1024]{3,2,1,0:T(2,128)(2,1)S(1)}, u32[]{:S(2)}, u32[]{:S(2)}) %collective-permute-start.4) | collective-permute-done | bytes 16416 | tf_op jit(solution)/shard_map/ppermute | solution.py:192
  29.2 0.0 copy-start.4
  29.2 0.0 collective-permute-done.3.other
  29.2 0.6 %copy-done.4 = bf16[2,2,2,1024]{3,2,1,0:T(2,128)(2,1)} copy-done((bf16[2,2,2,1024]{3,2,1,0:T(2,128)(2,1)}, bf16[2,2,2,1024]{3,2,1,0:T(2,128)(2,1)S(1)}, u32[]{:S(2)}) %copy-start.4) | copy-done | bytes 16408
  29.8 0.0 copy-start.1
  29.8 0.8 %copy-done.1 = bf16[2,2,64,1024]{3,2,1,0:T(8,128)(2,1)} copy-done((bf16[2,2,64,1024]{3,2,1,0:T(8,128)(2,1)}, bf16[2,2,64,1024]{3,2,1,0:T(8,128)(2,1)S(1)}, u32[]{:S(2)}) %copy-start.1) | copy-done | bytes 524312
  30.6 3.1 %stage_2.1.previous = bf16[2,4,64,1024]{3,2,1,0:T(8,128)(2,1)} custom-call(s32[2,4]{1,0:T(2,128)} %partners.3, s32[2]{0:T(128)} %counts.3, s32[2,4]{1,0:T(2,128)} %windows.3, bf16[2,2,64,1024]{3,2,1,0:T(8,128)(2,1)} %own.3, bf16[2,2,2,1024]{3,2,1,0:T(2,128)(2,1)} %copy-done.2, bf16[2,2,64,1024]{3,2,1,0:T(8,128)(2,1)} %copy-done.1, ...), custom_call_target="tpu_custom_call", output_to_operand_aliasing={{}: (7, {})} | custom-call | flops 1073741824 | bytes 4194304 | tf_op jit(solution)/shard_map/stage_2/pallas_call | solution.py:156
  33.7 0.0 collective-permute-done.2.other_edge
  33.7 0.0 copy-start.3
  33.7 0.0 collective-permute-done.1.other
  33.8 0.6 %copy-done.3 = bf16[2,2,2,1024]{3,2,1,0:T(2,128)(2,1)} copy-done((bf16[2,2,2,1024]{3,2,1,0:T(2,128)(2,1)}, bf16[2,2,2,1024]{3,2,1,0:T(2,128)(2,1)S(1)}, u32[]{:S(2)}) %copy-start.3) | copy-done | bytes 16408
  34.3 0.0 copy-start
  34.3 0.8 %copy-done = bf16[2,2,64,1024]{3,2,1,0:T(8,128)(2,1)} copy-done((bf16[2,2,64,1024]{3,2,1,0:T(8,128)(2,1)}, bf16[2,2,64,1024]{3,2,1,0:T(8,128)(2,1)S(1)}, u32[]{:S(2)}) %copy-start) | copy-done | bytes 524312
  35.1 4.3 %stage_4.1 = bf16[2,4,64,1024]{3,2,1,0:T(8,128)(2,1)} custom-call(s32[2,4]{1,0:T(2,128)} %partners.3, s32[2]{0:T(128)} %counts.3, s32[2,4]{1,0:T(2,128)} %windows.3, bf16[2,2,64,1024]{3,2,1,0:T(8,128)(2,1)} %own.3, bf16[2,2,2,1024]{3,2,1,0:T(2,128)(2,1)} %copy-done.2, bf16[2,2,64,1024]{3,2,1,0:T(8,128)(2,1)} %copy-done, ...), custom_call_target="tpu_custom_call", output_to_operand_aliasing={{}: (7, {})} | custom-call | flops 1073741824 | bytes 4194304 | tf_op jit(solution)/shard_map/stage_4/pallas_call | solution.py:156
Async XLA Ops:
  0.0 29.2 %collective-permute-start.3 = (bf16[2,2,64,1024]{3,2,1,0:T(8,128)(2,1)}, bf16[2,2,64,1024]{3,2,1,0:T(8,128)(2,1)S(1)}, u32[]{:S(2)}, u32[]{:S(2)}) collective-permute-start(bf16[2,2,64,1024]{3,2,1,0:T(8,128)(2,1)} %own.3), channel_id=1, source_target_pairs={{2,0},{4,2},{6,4},{8,6},{10,8},{12,10},{14,12},{0,14},{3,1},{5,3},... | collective-permute-start | bytes 1572872 | tf_op jit(solution)/shard_map/ppermute | solution.py:186
  6.0 27.7 %collective-permute-start.1 = (bf16[2,2,64,1024]{3,2,1,0:T(8,128)(2,1)}, bf16[2,2,64,1024]{3,2,1,0:T(8,128)(2,1)S(1)}, u32[]{:S(2)}, u32[]{:S(2)}) collective-permute-start(bf16[2,2,64,1024]{3,2,1,0:T(8,128)(2,1)} %own.3), channel_id=1, source_target_pairs={{4,0},{6,2},{8,4},{10,6},{12,8},{14,10},{0,12},{2,14},{5,1},{7,3},... | collective-permute-start | bytes 1572872 | tf_op jit(solution)/shard_map/ppermute | solution.py:186
  7.4 1.2 %collective-permute-start = (bf16[2,2,2,1024]{3,2,1,0:T(2,128)(2,1)S(1)}, bf16[2,2,2,1024]{3,2,1,0:T(2,128)(2,1)S(1)}, u32[]{:S(2)}, u32[]{:S(2)}) collective-permute-start(bf16[2,2,2,1024]{3,2,1,0:T(2,128)(2,1)S(1)} %broadcast_select_fusion), channel_id=1, source_target_pairs={{1,0},{0,1},{3,2},{2,3},{5,4},{4,5},{7,6},{6,7},{9,8},{8,9},{11,10... | collective-permute-start | bytes 49160 | tf_op jit(solution)/shard_map/ppermute | solution.py:192
  7.5 21.7 %collective-permute-start.4 = (bf16[2,2,2,1024]{3,2,1,0:T(2,128)(2,1)S(1)}, bf16[2,2,2,1024]{3,2,1,0:T(2,128)(2,1)S(1)}, u32[]{:S(2)}, u32[]{:S(2)}) collective-permute-start(bf16[2,2,2,1024]{3,2,1,0:T(2,128)(2,1)S(1)} %broadcast_select_fusion), channel_id=1, source_target_pairs={{3,0},{2,1},{5,2},{4,3},{7,4},{6,5},{9,6},{8,7},{11,8},{10,9},{13,... | collective-permute-start | bytes 49160 | tf_op jit(solution)/shard_map/ppermute | solution.py:192
  8.1 25.7 %collective-permute-start.2 = (bf16[2,2,2,1024]{3,2,1,0:T(2,128)(2,1)S(1)}, bf16[2,2,2,1024]{3,2,1,0:T(2,128)(2,1)S(1)}, u32[]{:S(2)}, u32[]{:S(2)}) collective-permute-start(bf16[2,2,2,1024]{3,2,1,0:T(2,128)(2,1)S(1)} %broadcast_select_fusion), channel_id=1, source_target_pairs={{5,0},{4,1},{7,2},{6,3},{9,4},{8,5},{11,6},{10,7},{13,8},{12,9},{1... | collective-permute-start | bytes 49160 | tf_op jit(solution)/shard_map/ppermute | solution.py:192
  8.6 0.6 %copy-start.2 = (bf16[2,2,2,1024]{3,2,1,0:T(2,128)(2,1)}, bf16[2,2,2,1024]{3,2,1,0:T(2,128)(2,1)S(1)}, u32[]{:S(2)}) copy-start(bf16[2,2,2,1024]{3,2,1,0:T(2,128)(2,1)S(1)} %collective-permute-done.refs_4_.refs_6_.own_edge) | copy-start | bytes 49156
  29.2 0.6 %copy-start.4 = (bf16[2,2,2,1024]{3,2,1,0:T(2,128)(2,1)}, bf16[2,2,2,1024]{3,2,1,0:T(2,128)(2,1)S(1)}, u32[]{:S(2)}) copy-start(bf16[2,2,2,1024]{3,2,1,0:T(2,128)(2,1)S(1)} %collective-permute-done.4.other_edge) | copy-start | bytes 49156
  29.8 0.8 %copy-start.1 = (bf16[2,2,64,1024]{3,2,1,0:T(8,128)(2,1)}, bf16[2,2,64,1024]{3,2,1,0:T(8,128)(2,1)S(1)}, u32[]{:S(2)}) copy-start(bf16[2,2,64,1024]{3,2,1,0:T(8,128)(2,1)S(1)} %collective-permute-done.3.other) | copy-start | bytes 1572868
  33.7 0.6 %copy-start.3 = (bf16[2,2,2,1024]{3,2,1,0:T(2,128)(2,1)}, bf16[2,2,2,1024]{3,2,1,0:T(2,128)(2,1)S(1)}, u32[]{:S(2)}) copy-start(bf16[2,2,2,1024]{3,2,1,0:T(2,128)(2,1)S(1)} %collective-permute-done.2.other_edge) | copy-start | bytes 49156
  34.3 0.8 %copy-start = (bf16[2,2,64,1024]{3,2,1,0:T(8,128)(2,1)}, bf16[2,2,64,1024]{3,2,1,0:T(8,128)(2,1)S(1)}, u32[]{:S(2)}) copy-start(bf16[2,2,64,1024]{3,2,1,0:T(8,128)(2,1)S(1)} %collective-permute-done.1.other) | copy-start | bytes 1572868

commit v2 on v1

--- a/solution.py
+++ b/solution.py
@@ -7,7 +7,7 @@
 from jax.experimental.pallas import tpu as pltpu
 from jax.sharding import PartitionSpec as P
 
-REACH_COLS = 5
+
 HALO = 2
 LANES = 128
 TOP = 8
@@ -16,10 +16,9 @@
 
 def stage_kernel(
     first_local,
+    edge_start,
     fill,
-    total_dates,
-    partners,
-    counts,
+    ahead_of,
     windows,
     own,
     own_edge,
@@ -37,18 +36,16 @@
     del previous
     dates_dev, _, rows, cols = own.shape
     here = other.shape[0]
-    per_date = partners.shape[1]
+    per_date = windows.shape[1]
     slots = dates_dev * per_date
     stripes = cols // LANES
-    first_date = lax.axis_index("date") * dates_dev
     upper = lax.axis_index("row") == 0
 
     def state(slot):
         date, place = slot // per_date, slot % per_date
-        ahead = lax.rem(partners[date, place] - first_date + total_dates, total_dates) - first_local
-        used = place < counts[date]
-        mine = jnp.logical_and(used, jnp.logical_and(ahead >= 0, ahead < here))
-        return date, place, jnp.clip(ahead, 0, here - 1), used, mine
+        ahead = ahead_of[date, place]
+        mine = jnp.logical_and(ahead >= first_local, ahead < first_local + here)
+        return date, place, ahead, mine
 
     def copy_of(slot, source):
         return pltpu.make_async_copy(source, out.at[slot // per_date, slot % per_date], sems.at[slot])
@@ -59,9 +56,9 @@
         zeros[...] = jnp.zeros_like(zeros)
 
         def clear(slot, carry):
-            _, _, _, used, _ = state(slot)
-
-            @pl.when(jnp.logical_not(used))
+            _, _, ahead, _ = state(slot)
+
+            @pl.when(ahead < 0)
             def _():
                 copy_of(slot, zeros).start()
 
@@ -80,19 +77,20 @@
         )
 
     def one_slot(slot, carry):
-        date, place, ahead, _, mine = state(slot)
+        date, place, ahead, mine = state(slot)
 
         @pl.when(mine)
         def _():
+            there = ahead - first_local
             half_width = windows[date, place]
             depth = lax.broadcasted_iota(jnp.int32, band.shape, 0)
             width = lax.broadcasted_iota(jnp.int32, band.shape, 1)
             band[...] = jnp.where(jnp.abs(depth - LANES - width) <= half_width, 1.0, 0.0).astype(jnp.bfloat16)
             for stripe in range(stripes):
                 at = slice(stripe * LANES, (stripe + 1) * LANES)
-                main = planes(own[date, 0, :, at], own[date, 1, :, at], other[ahead, 0, :, at], other[ahead, 1, :, at])
+                main = planes(own[date, 0, :, at], own[date, 1, :, at], other[there, 0, :, at], other[there, 1, :, at])
                 edge = planes(
-                    own_edge[date, 0, :, at], own_edge[date, 1, :, at], other_edge[ahead, 0, :, at], other_edge[ahead, 1, :, at]
+                    own_edge[date, 0, :, at], own_edge[date, 1, :, at], other_edge[edge_start + there, 0, :, at], other_edge[edge_start + there, 1, :, at]
                 )
                 for k in range(4):
                     products[k, TOP : TOP + rows, :] = main[k]
@@ -124,8 +122,8 @@
     lax.fori_loop(0, slots, one_slot, 0)
 
     def finish(slot, carry):
-        _, _, _, used, mine = state(slot)
-        started = jnp.logical_or(mine, jnp.logical_not(used)) if fill else mine
+        _, _, ahead, mine = state(slot)
+        started = jnp.logical_or(mine, ahead < 0) if fill else mine
 
         @pl.when(started)
         def _():
@@ -136,18 +134,18 @@
     lax.fori_loop(0, slots, finish, 0)
 
 
-def stage(first_local, total_dates, tables, own, own_edge, other, other_edge, previous):
+def stage(first_local, tables, own, own_edge, other, other_edge, edge_start, previous):
     dates_dev, _, rows, cols = own.shape
-    per_date = tables[0].shape[1]
+    per_date = tables[1].shape[1]
     slots = dates_dev * per_date
     shape = jax.ShapeDtypeStruct((dates_dev, per_date, rows, cols), jnp.bfloat16)
     fill = previous is None
-    kernel = functools.partial(stage_kernel, first_local, fill, total_dates)
+    kernel = functools.partial(stage_kernel, first_local, edge_start, fill)
     if fill:
         inner = kernel
 
         def kernel(*refs):
-            inner(*refs[:7], None, *refs[7:])
+            inner(*refs[:6], None, *refs[6:])
 
     smem = pl.BlockSpec(memory_space=pltpu.SMEM)
     vmem = pl.BlockSpec(memory_space=pltpu.VMEM)
@@ -156,7 +154,7 @@
     return pl.pallas_call(
         kernel,
         out_shape=shape,
-        in_specs=[smem] * 3 + [vmem] * 4 + ([] if fill else [anywhere]),
+        in_specs=[smem] * 2 + [vmem] * 4 + ([] if fill else [anywhere]),
         out_specs=anywhere,
         scratch_shapes=[
             pltpu.VMEM((4, rows + 2 * TOP, LANES), jnp.float32),
@@ -166,35 +164,59 @@
             pltpu.VMEM((rows, cols), jnp.bfloat16),
             pltpu.SemaphoreType.DMA((slots,)),
         ],
-        input_output_aliases={} if fill else {7: 0},
-        name=f"stage_{first_local}",
+        input_output_aliases={} if fill else {6: 0},
+        compiler_params=pltpu.CompilerParams(vmem_limit_bytes=16 << 20),
         cost_estimate=pl.CostEstimate(flops=1 << 30, bytes_accessed=1 << 22, transcendentals=0),
     )(*tables, own, own_edge, other, other_edge, *([] if fill else [previous]))
 
 
-def local(slc_stack, partners, counts, windows):
+def relayed(slc_stack, edges, loop_size):
+    first, second = slc_stack[0:1], lax.optimization_barrier(slc_stack)[1:2]
+    by_two = [((i + 2) % loop_size, i) for i in range(loop_size)]
+    by_one = [((i + 1) % loop_size, i) for i in range(loop_size)]
+    far_first = lax.ppermute(first, "date", by_two)
+    near_second = lax.ppermute(second, "date", by_one)
+    far_second = lax.ppermute(second, "date", by_two)
+    near_direct = lax.ppermute(first, "date", [(i + 1, i) for i in range(0, loop_size, 2)])
+    near_relayed = lax.ppermute(far_first, "date", [(i - 1, i) for i in range(1, loop_size, 2)])
+    odd = lax.rem(lax.axis_index("date"), 2) == 1
+    near_first = jnp.where(odd, near_relayed, near_direct)
+    return [
+        (4, far_first, edges[2], 0),
+        (3, near_second, edges[1], 1),
+        (2, near_first, edges[1], 0),
+        (5, far_second, edges[2], 1),
+    ]
+
+
+def whole(slc_stack, partners, counts, windows):
     dates_dev, _, rows, _ = slc_stack.shape
     loop_size = lax.axis_size("date")
     strips = lax.axis_size("row")
     assert strips == 2
     reach = loop_size // 4
     total_dates = dates_dev * loop_size
-    tables = (partners, counts, windows)
+    first_date = lax.axis_index("date") * dates_dev
+    ahead_of = jnp.where(partners < first_date, partners + total_dates, partners) - first_date
+    used = lax.broadcasted_iota(jnp.int32, partners.shape, 1) < counts[:, None]
+    tables = (jnp.where(used, ahead_of, -1), windows)
     edge = jnp.where(lax.axis_index("row") == 0, slc_stack[:, :, rows - HALO :], slc_stack[:, :, :HALO])
-    blocks = []
-    for distance in range(1, reach + 1):
-        blocks.append(lax.ppermute(slc_stack, "date", [((i + distance) % loop_size, i) for i in range(loop_size)]))
     edges = []
     for distance in range(reach + 1):
         pairs = [
             (((i + distance) % loop_size) * strips + (1 - r), i * strips + r) for i in range(loop_size) for r in range(strips)
         ]
         edges.append(lax.ppermute(edge, ("date", "row"), pairs))
-    out = stage(0, total_dates, tables, slc_stack, edges[0], slc_stack, edges[0], None)
-    for distance in range(1, reach + 1):
-        out = stage(
-            distance * dates_dev, total_dates, tables, slc_stack, edges[0], blocks[distance - 1], edges[distance], out
-        )
+    out = stage(0, tables, slc_stack, edges[0], slc_stack, edges[0], 0, None)
+    if reach == 2 and dates_dev == 2:
+        arrivals = relayed(slc_stack, edges, loop_size)
+    else:
+        arrivals = []
+        for distance in range(1, reach + 1):
+            block = lax.ppermute(slc_stack, "date", [((i + distance) % loop_size, i) for i in range(loop_size)])
+            arrivals.append((distance * dates_dev, block, edges[distance], 0))
+    for first_local, block, block_edge, edge_start in arrivals:
+        out = stage(first_local, tables, slc_stack, edges[0], block, block_edge, edge_start, out)
     return out
 
 
@@ -206,4 +228,4 @@
         P("date", None),
     )
     out_specs = P("date", None, ("tiles", "row"), None)
-    return jax.shard_map(local, mesh=mesh, in_specs=in_specs, out_specs=out_specs, check_vma=False)
+    return jax.shard_map(whole, mesh=mesh, in_specs=in_specs, out_specs=out_specs, check_vma=False)

time: 39.7 us -> 31 us (0.78)
  waiting for transfers between devices: 18.1 us -> 2.28 us
  starting transfers between devices: 7.28 us -> 16.6 us
  local copies, waits for them, and re-layouts: 3.38 us -> 1.74 us
  other arithmetic: 0.9 us -> 0.14 us
    ppermute x5 -> x8, waiting for transfers between devices: 18.1 us -> 2.28 us  [the longest x1 2.27 us: relayed(): far_first = lax.ppermute(first, 'date', by_two)]
    ppermute x5 -> x8, starting transfers between devices: 7.28 us -> 16.6 us  [the longest x1 5.41 us: relayed(): far_second = lax.ppermute(second, 'date', by_two)]
    unnamed x10 -> x8, local copies, waits for them, and re-layouts: 3.38 us -> 0.69 us
    slice x0 -> x2, local copies, waits for them, and re-layouts: none -> 1.06 us  [relayed(): first, second = (slc_stack[0:1], lax.optimization_barrier(slc_stack)[1:2])]
    select_n x1 -> x3, other arithmetic: 0.9 us -> 0.14 us  [the longest x1 0.07 us: whole(): tables = (jnp.where(used, ahead_of, -1), windows)]
    pallas_call x3 -> x5, Pallas kernels: 9.68 us -> 9.94 us  [stage(): pl.pallas_call(kernel, out_shape=shape, in_specs=[smem] * 2 + [vmem] * 4...]
  transfers between devices with their start and end apart: 5 -> 8, of which waited for: 2 -> 1; matrix products, arithmetic and copies ran while one was open for 2% -> 0% of each run, Pallas kernels for 14% -> 24%
where the time goes in v2:
time: 31 us; the launch traced here: 30.8 us
  starting transfers between devices  16.6 us (54%)
  Pallas kernels  9.94 us (32%)
  waiting for transfers between devices  2.28 us (7%)
  local copies, waits for them, and re-layouts  1.74 us (6%)
    pallas_call x5, Pallas kernels, stage(): pl.pallas_call(kernel, out_shape=shape, in_specs=[smem] * 2 + [vmem] * 4...  9.94 us
    ppermute x1, starting transfers between devices, relayed(): far_second = lax.ppermute(second, 'date', by_two)  5.41 us
    ppermute x1, starting transfers between devices, relayed(): far_first = lax.ppermute(first, 'date', by_two)  5.13 us
    ppermute x1, starting transfers between devices, relayed(): lax.ppermute(far_first, 'date', [(i - 1, i) for i in range(1, loop_size,...  2.47 us
    ppermute x1, waiting for transfers between devices, relayed(): far_first = lax.ppermute(first, 'date', by_two)  2.27 us
    ppermute x3, starting transfers between devices, whole(): edges.append(lax.ppermute(edge, ('date', 'row'), pairs))  1.63 us
    ppermute x1, starting transfers between devices, relayed(): lax.ppermute(first, 'date', [(i + 1, i) for i in range(0, loop_size, 2)])  1.41 us
    slice x2, local copies, waits for them, and re-layouts, relayed(): first, second = (slc_stack[0:1], lax.optimization_barrier(slc_stack)[1:2])  1.06 us
  transfers between devices with their start and end apart: 8, of which 1 were waited for; matrix products, arithmetic and copies ran while one was open for 0% of the time, Pallas kernels for 24%

profile of v2, /device:TPU:0, one launch (start us, length us, event | category | flops | bytes accessed | tf_op | source)
XLA Modules:
  0.0 30.8 jit_solution(12661721699535562045)
XLA Ops:
  0.0 1.0 %slice.15 = bf16[1,2,64,1024]{3,2,1,0:T(8,128)(2,1)S(1)} slice(bf16[2,2,64,1024]{3,2,1,0:T(8,128)(2,1)} %own.7), slice={[0:1], [0:2], [0:64], [0:1024]} | slice | bytes 524288 | tf_op jit(solution)/shard_map/slice | solution.py:174
  1.0 5.1 %collective-permute-start.3 = (bf16[1,2,64,1024]{3,2,1,0:T(8,128)(2,1)S(1)}, bf16[1,2,64,1024]{3,2,1,0:T(8,128)(2,1)S(1)}, u32[]{:S(2)}, u32[]{:S(2)}) collective-permute-start(bf16[1,2,64,1024]{3,2,1,0:T(8,128)(2,1)S(1)} %slice.15), channel_id=1, source_target_pairs={{4,0},{6,2},{8,4},{10,6},{12,8},{14,10},{0,12},{2,14},{5,1},{7,3},... | collective-permute-start | bytes 786440 | tf_op jit(solution)/shard_map/ppermute | solution.py:177
  6.2 0.6 %collective-permute-start.6 = (bf16[2,2,2,1024]{3,2,1,0:T(2,128)(2,1)S(1)}, bf16[2,2,2,1024]{3,2,1,0:T(2,128)(2,1)S(1)}, u32[]{:S(2)}, u32[]{:S(2)}) collective-permute-start(bf16[2,2,2,1024]{3,2,1,0:T(2,128)(2,1)S(1)} %broadcast_select_fusion.1), channel_id=1, source_target_pairs={{3,0},{2,1},{5,2},{4,3},{7,4},{6,5},{9,6},{8,7},{11,8},{10,9},{13,... | collective-permute-start | bytes 49160 | tf_op jit(solution)/shard_map/ppermute | solution.py:209
  6.8 1.0 %collective-permute-start.2 = (bf16[2,2,2,1024]{3,2,1,0:T(2,128)(2,1)S(1)}, bf16[2,2,2,1024]{3,2,1,0:T(2,128)(2,1)S(1)}, u32[]{:S(2)}, u32[]{:S(2)}) collective-permute-start(bf16[2,2,2,1024]{3,2,1,0:T(2,128)(2,1)S(1)} %broadcast_select_fusion.1), channel_id=1, source_target_pairs={{5,0},{4,1},{7,2},{6,3},{9,4},{8,5},{11,6},{10,7},{13,8},{12,9},{1... | collective-permute-start | bytes 49160 | tf_op jit(solution)/shard_map/ppermute | solution.py:209
  7.8 0.0 collective-permute-start
  7.9 0.6 %collective-permute-start.7 = (bf16[1,2,64,1024]{3,2,1,0:T(8,128)(2,1)S(1)}, bf16[1,2,64,1024]{3,2,1,0:T(8,128)(2,1)S(1)}, u32[]{:S(2)}, u32[]{:S(2)}) collective-permute-start(bf16[1,2,64,1024]{3,2,1,0:T(8,128)(2,1)S(1)} %slice.16), channel_id=1, source_target_pairs={{2,0},{4,2},{6,4},{8,6},{10,8},{12,10},{14,12},{0,14},{3,1},{5,3},... | collective-permute-start | bytes 786440 | tf_op jit(solution)/shard_map/ppermute | solution.py:178
  8.4 0.7 %copy-done.2 = s32[2,4]{1,0:T(2,128)S(1)} copy-done((s32[2,4]{1,0:T(2,128)S(1)}, s32[2,4]{1,0:T(2,128)}, u32[]{:S(2)}) %copy-start.2) | copy-done | bytes 56
  9.1 0.1 compare_select_fusion.1.refs_0_.ahead_of
  9.2 0.0 collective-permute-done.refs_3_.refs_5_.own_edge
  9.2 1.4 %collective-permute-start.5 = (bf16[1,2,64,1024]{3,2,1,0:T(8,128)(2,1)S(1)}, bf16[1,2,64,1024]{3,2,1,0:T(8,128)(2,1)S(1)}, u32[]{:S(2)}, u32[]{:S(2)}) collective-permute-start(bf16[1,2,64,1024]{3,2,1,0:T(8,128)(2,1)S(1)} %slice.15), channel_id=1, source_target_pairs={{2,0},{6,4},{10,8},{14,12},{3,1},{7,5},{11,9},{15,13},{18,16},{22,... | collective-permute-start | bytes 786440 | tf_op jit(solution)/shard_map/ppermute | solution.py:180
  10.6 2.3 %collective-permute-done.3.other = bf16[1,2,64,1024]{3,2,1,0:T(8,128)(2,1)S(1)} collective-permute-done((bf16[1,2,64,1024]{3,2,1,0:T(8,128)(2,1)S(1)}, bf16[1,2,64,1024]{3,2,1,0:T(8,128)(2,1)S(1)}, u32[]{:S(2)}, u32[]{:S(2)}) %collective-permute-start.3) | collective-permute-done | bytes 262176 | tf_op jit(solution)/shard_map/ppermute | solution.py:177
  12.9 2.5 %collective-permute-start.4 = (bf16[1,2,64,1024]{3,2,1,0:T(8,128)(2,1)S(1)}, bf16[1,2,64,1024]{3,2,1,0:T(8,128)(2,1)S(1)}, u32[]{:S(2)}, u32[]{:S(2)}) collective-permute-start(bf16[1,2,64,1024]{3,2,1,0:T(8,128)(2,1)S(1)} %collective-permute-done.3.other), channel_id=1, source_target_pairs={{0,2},{4,6},{8,10},{12,14},{1,3},{5,7},{9,11},{13,15},{16,18},{20,... | collective-permute-start | bytes 786440 | tf_op jit(solution)/shard_map/ppermute | solution.py:181
  15.4 1.5 %shard_map.46.previous = bf16[2,4,64,1024]{3,2,1,0:T(8,128)(2,1)} custom-call(s32[2,4]{1,0:T(2,128)S(1)} %compare_select_fusion.1.refs_0_.ahead_of, s32[2,4]{1,0:T(2,128)S(1)} %copy-done.1, bf16[2,2,64,1024]{3,2,1,0:T(8,128)(2,1)S(1)} %copy-done, bf16[2,2,2,1024]{3,2,1,0:T(2,128)(2,1)S(1)} %collective-permute-done.refs_3_.refs_5_.own_edge, ...), custom_call_target="tpu_custom_call" | custom-call | flops 1073741824 | bytes 4194304 | tf_op jit(solution)/shard_map/pallas_call | solution.py:154
  16.9 0.0 collective-permute-done.2.other_edge
  16.9 5.4 %collective-permute-start.1 = (bf16[1,2,64,1024]{3,2,1,0:T(8,128)(2,1)S(1)}, bf16[1,2,64,1024]{3,2,1,0:T(8,128)(2,1)S(1)}, u32[]{:S(2)}, u32[]{:S(2)}) collective-permute-start(bf16[1,2,64,1024]{3,2,1,0:T(8,128)(2,1)S(1)} %slice.16), channel_id=1, source_target_pairs={{4,0},{6,2},{8,4},{10,6},{12,8},{14,10},{0,12},{2,14},{5,1},{7,3},... | collective-permute-start | bytes 786440 | tf_op jit(solution)/shard_map/ppermute | solution.py:179
  22.3 2.4 %shard_map.47.previous = bf16[2,4,64,1024]{3,2,1,0:T(8,128)(2,1)} custom-call(s32[2,4]{1,0:T(2,128)S(1)} %compare_select_fusion.1.refs_0_.ahead_of, s32[2,4]{1,0:T(2,128)S(1)} %copy-done.1, bf16[2,2,64,1024]{3,2,1,0:T(8,128)(2,1)S(1)} %copy-done, ...), custom_call_target="tpu_custom_call", output_to_operand_aliasing={{}: (6, {})} | custom-call | flops 1073741824 | bytes 4194304 | tf_op jit(solution)/shard_map/pallas_call | solution.py:154
  24.8 0.0 collective-permute-done.6.other_edge
  24.8 0.0 collective-permute-done.7.other
  24.8 1.0 %shard_map.48.previous = bf16[2,4,64,1024]{3,2,1,0:T(8,128)(2,1)} custom-call(s32[2,4]{1,0:T(2,128)S(1)} %compare_select_fusion.1.refs_0_.ahead_of, s32[2,4]{1,0:T(2,128)S(1)} %copy-done.1, bf16[2,2,64,1024]{3,2,1,0:T(8,128)(2,1)S(1)} %copy-done, ...), custom_call_target="tpu_custom_call", output_to_operand_aliasing={{}: (6, {})} | custom-call | flops 1073741824 | bytes 4194304 | tf_op jit(solution)/shard_map/pallas_call | solution.py:154
  25.8 0.0 collective-permute-done.5
  25.8 0.0 collective-permute-done.4
  25.9 2.4 %shard_map.49.previous = bf16[2,4,64,1024]{3,2,1,0:T(8,128)(2,1)} custom-call(s32[2,4]{1,0:T(2,128)S(1)} %compare_select_fusion.1.refs_0_.ahead_of, s32[2,4]{1,0:T(2,128)S(1)} %copy-done.1, bf16[2,2,64,1024]{3,2,1,0:T(8,128)(2,1)S(1)} %copy-done, ...), custom_call_target="tpu_custom_call", output_to_operand_aliasing={{}: (6, {})} | custom-call | flops 1073741824 | bytes 4194304 | tf_op jit(solution)/shard_map/pallas_call | solution.py:154
  28.3 0.0 collective-permute-done.1.other
  28.3 2.5 %shard_map.50 = bf16[2,4,64,1024]{3,2,1,0:T(8,128)(2,1)} custom-call(s32[2,4]{1,0:T(2,128)S(1)} %compare_select_fusion.1.refs_0_.ahead_of, s32[2,4]{1,0:T(2,128)S(1)} %copy-done.1, bf16[2,2,64,1024]{3,2,1,0:T(8,128)(2,1)S(1)} %copy-done, bf16[2,2,2,1024]{3,2,1,0:T(2,128)(2,1)S(1)} %collective-permute-done.refs_3_.refs_5_.own_edge, ...), custom_call_target="tpu_custom_call", output_to_operand_aliasing={{}: (6, {})} | custom-call | flops 1073741824 | bytes 4194304 | tf_op jit(solution)/shard_map/pallas_call | solution.py:154
  (10 shorter events, 0.1 us)
Async XLA Ops:
  0.0 6.2 %copy-start = (bf16[2,2,64,1024]{3,2,1,0:T(8,128)(2,1)S(1)}, bf16[2,2,64,1024]{3,2,1,0:T(8,128)(2,1)}, u32[]{:S(2)}) copy-start(bf16[2,2,64,1024]{3,2,1,0:T(8,128)(2,1)} %own.7) | copy-start | bytes 1572868
  1.0 11.8 %collective-permute-start.3 = (bf16[1,2,64,1024]{3,2,1,0:T(8,128)(2,1)S(1)}, bf16[1,2,64,1024]{3,2,1,0:T(8,128)(2,1)S(1)}, u32[]{:S(2)}, u32[]{:S(2)}) collective-permute-start(bf16[1,2,64,1024]{3,2,1,0:T(8,128)(2,1)S(1)} %slice.15), channel_id=1, source_target_pairs={{4,0},{6,2},{8,4},{10,6},{12,8},{14,10},{0,12},{2,14},{5,1},{7,3},... | collective-permute-start | bytes 786440 | tf_op jit(solution)/shard_map/ppermute | solution.py:177
  6.2 18.6 %collective-permute-start.6 = (bf16[2,2,2,1024]{3,2,1,0:T(2,128)(2,1)S(1)}, bf16[2,2,2,1024]{3,2,1,0:T(2,128)(2,1)S(1)}, u32[]{:S(2)}, u32[]{:S(2)}) collective-permute-start(bf16[2,2,2,1024]{3,2,1,0:T(2,128)(2,1)S(1)} %broadcast_select_fusion.1), channel_id=1, source_target_pairs={{3,0},{2,1},{5,2},{4,3},{7,4},{6,5},{9,6},{8,7},{11,8},{10,9},{13,... | collective-permute-start | bytes 49160 | tf_op jit(solution)/shard_map/ppermute | solution.py:209
  6.8 10.1 %collective-permute-start.2 = (bf16[2,2,2,1024]{3,2,1,0:T(2,128)(2,1)S(1)}, bf16[2,2,2,1024]{3,2,1,0:T(2,128)(2,1)S(1)}, u32[]{:S(2)}, u32[]{:S(2)}) collective-permute-start(bf16[2,2,2,1024]{3,2,1,0:T(2,128)(2,1)S(1)} %broadcast_select_fusion.1), channel_id=1, source_target_pairs={{5,0},{4,1},{7,2},{6,3},{9,4},{8,5},{11,6},{10,7},{13,8},{12,9},{1... | collective-permute-start | bytes 49160 | tf_op jit(solution)/shard_map/ppermute | solution.py:209
  7.8 1.3 %collective-permute-start = (bf16[2,2,2,1024]{3,2,1,0:T(2,128)(2,1)S(1)}, bf16[2,2,2,1024]{3,2,1,0:T(2,128)(2,1)S(1)}, u32[]{:S(2)}, u32[]{:S(2)}) collective-permute-start(bf16[2,2,2,1024]{3,2,1,0:T(2,128)(2,1)S(1)} %broadcast_select_fusion.1), channel_id=1, source_target_pairs={{1,0},{0,1},{3,2},{2,3},{5,4},{4,5},{7,6},{6,7},{9,8},{8,9},{11,10... | collective-permute-start | bytes 49160 | tf_op jit(solution)/shard_map/ppermute | solution.py:209
  7.9 16.9 %collective-permute-start.7 = (bf16[1,2,64,1024]{3,2,1,0:T(8,128)(2,1)S(1)}, bf16[1,2,64,1024]{3,2,1,0:T(8,128)(2,1)S(1)}, u32[]{:S(2)}, u32[]{:S(2)}) collective-permute-start(bf16[1,2,64,1024]{3,2,1,0:T(8,128)(2,1)S(1)} %slice.16), channel_id=1, source_target_pairs={{2,0},{4,2},{6,4},{8,6},{10,8},{12,10},{14,12},{0,14},{3,1},{5,3},... | collective-permute-start | bytes 786440 | tf_op jit(solution)/shard_map/ppermute | solution.py:178
  8.4 0.7 %copy-start.2 = (s32[2,4]{1,0:T(2,128)S(1)}, s32[2,4]{1,0:T(2,128)}, u32[]{:S(2)}) copy-start(s32[2,4]{1,0:T(2,128)} %param.5) | copy-start | bytes 100
  8.4 0.7 %copy-start.3 = (s32[2]{0:T(128)S(1)}, s32[2]{0:T(128)}, u32[]{:S(2)}) copy-start(s32[2]{0:T(128)} %param.6) | copy-start | bytes 28
  9.2 6.2 %copy-start.1 = (s32[2,4]{1,0:T(2,128)S(1)}, s32[2,4]{1,0:T(2,128)}, u32[]{:S(2)}) copy-start(s32[2,4]{1,0:T(2,128)} %windows.7) | copy-start | bytes 100
  9.2 16.6 %collective-permute-start.5 = (bf16[1,2,64,1024]{3,2,1,0:T(8,128)(2,1)S(1)}, bf16[1,2,64,1024]{3,2,1,0:T(8,128)(2,1)S(1)}, u32[]{:S(2)}, u32[]{:S(2)}) collective-permute-start(bf16[1,2,64,1024]{3,2,1,0:T(8,128)(2,1)S(1)} %slice.15), channel_id=1, source_target_pairs={{2,0},{6,4},{10,8},{14,12},{3,1},{7,5},{11,9},{15,13},{18,16},{22,... | collective-permute-start | bytes 786440 | tf_op jit(solution)/shard_map/ppermute | solution.py:180
  12.9 12.9 %collective-permute-start.4 = (bf16[1,2,64,1024]{3,2,1,0:T(8,128)(2,1)S(1)}, bf16[1,2,64,1024]{3,2,1,0:T(8,128)(2,1)S(1)}, u32[]{:S(2)}, u32[]{:S(2)}) collective-permute-start(bf16[1,2,64,1024]{3,2,1,0:T(8,128)(2,1)S(1)} %collective-permute-done.3.other), channel_id=1, source_target_pairs={{0,2},{4,6},{8,10},{12,14},{1,3},{5,7},{9,11},{13,15},{16,18},{20,... | collective-permute-start | bytes 786440 | tf_op jit(solution)/shard_map/ppermute | solution.py:181
  16.9 11.4 %collective-permute-start.1 = (bf16[1,2,64,1024]{3,2,1,0:T(8,128)(2,1)S(1)}, bf16[1,2,64,1024]{3,2,1,0:T(8,128)(2,1)S(1)}, u32[]{:S(2)}, u32[]{:S(2)}) collective-permute-start(bf16[1,2,64,1024]{3,2,1,0:T(8,128)(2,1)S(1)} %slice.16), channel_id=1, source_target_pairs={{4,0},{6,2},{8,4},{10,6},{12,8},{14,10},{0,12},{2,14},{5,1},{7,3},... | collective-permute-start | bytes 786440 | tf_op jit(solution)/shard_map/ppermute | solution.py:179

commit v3 on v0

v3 whole, which is shorter than its diff:
```python
import functools

import jax
import jax.numpy as jnp
from jax import lax
from jax.experimental import pallas as pl
from jax.experimental.pallas import tpu as pltpu
from jax.sharding import PartitionSpec as P


NARROW = 3
WIDE = 5
HALO = 2
LANES = 128
BLOCK = 2 * LANES
TOP = 8
SMALLEST = 1.1754944e-38
CODE = 8


def band_table():
    shape = (WIDE - NARROW + 1, 2 * BLOCK, BLOCK)
    width = lax.broadcasted_iota(jnp.int32, shape, 0) + NARROW
    off = lax.broadcasted_iota(jnp.int32, shape, 1) - LANES - lax.broadcasted_iota(jnp.int32, shape, 2)
    return jnp.where(jnp.abs(off) <= width, 1.0, 0.0).astype(jnp.bfloat16)


def stage_kernel(role, rows_of, layout, span, places, final_rows, blocks, *refs):
    table, bands, own, own_edge, *refs = refs
    other, refs = refs[:blocks], refs[blocks:]
    dates_dev, _, rows, cols = own.shape
    here = len(rows_of)
    stripes = cols // LANES
    wide = BLOCK // LANES
    near_stripes = range(max(0, span[0] * wide - 1), min(stripes, span[1] * wide + 1))
    upper = lax.axis_index("row") == 0
    if role == "first":
        results, own_box, products, split, other_power = refs
    elif role == "middle":
        own_box, results, products, split, other_power = refs
    elif role == "gather":
        own_box, *refs = refs
        earlier, refs = refs[: len(places)], refs[len(places) :]
        out, products, split, other_power, results, sems, zeros, zero_sems = refs
    else:
        own_box, _, out, products, split, other_power, results, sems = refs
    codes = table[...]

    def pad(ref, at):
        if span[0] == 0:
            ref[at, :, 0:LANES] = jnp.zeros((ref.shape[1], LANES), jnp.bfloat16)
        if span[1] * BLOCK == cols:
            ref[at, :, LANES + cols :] = jnp.zeros((ref.shape[1], LANES), jnp.bfloat16)

    def over_rows(ref, at, stripe, k, main, edge):
        products[k, TOP : TOP + rows, :] = main
        products[k, TOP - HALO : TOP, :] = jnp.where(upper, 0.0, edge)
        products[k, TOP + rows : TOP + rows + HALO, :] = jnp.where(upper, edge, 0.0)
        total = products[k, TOP - HALO : TOP - HALO + rows, :]
        for shift in range(1, 2 * HALO + 1):
            total = total + products[k, TOP - HALO + shift : TOP - HALO + shift + rows, :]
        high = total.astype(jnp.bfloat16)
        low = (total - high.astype(jnp.float32)).astype(jnp.bfloat16)
        into = slice(LANES + stripe * LANES, LANES + (stripe + 1) * LANES)
        ref[at, 2 * k * rows : (2 * k + 1) * rows, into] = high
        ref[at, (2 * k + 1) * rows : (2 * k + 2) * rows, into] = low

    def stripe_of(ref, at, stripe):
        columns = slice(stripe * LANES, (stripe + 1) * LANES)
        return tuple(ref[at, plane, :, columns].astype(jnp.float32) for plane in range(2))

    def own_stripe(date, stripe):
        return *stripe_of(own, date, stripe), *stripe_of(own_edge, date, stripe)

    def other_stripe(t, stripe):
        if layout is None:
            return *stripe_of(other[0], t, stripe), *stripe_of(other[1], t, stripe)
        found = []
        for (k, start, base), size in zip(layout(stripe), (rows, rows, HALO, HALO)):
            if len(other[k].shape) == 4:
                found.append(other[k][start, base, :, stripe * LANES : (stripe + 1) * LANES].astype(jnp.float32))
                continue
            columns = slice((stripe - base) * LANES, (stripe - base + 1) * LANES)
            found.append(other[k][0, start : start + size, columns].astype(jnp.float32))
        return found

    def fill_power(ref, at, source, source_at):
        pad(ref, at)
        for stripe in near_stripes:
            re, im, edge_re, edge_im = source(source_at, stripe)
            over_rows(ref, at, stripe, 0, re * re + im * im, edge_re * edge_re + edge_im * edge_im)

    def over_columns(parts, width):
        box = jnp.dot(jnp.concatenate(parts, axis=0), bands[width], preferred_element_type=jnp.float32)
        return [box[k : k + rows] + box[k + rows : k + 2 * rows] for k in range(0, box.shape[0], 2 * rows)]

    def fill_box(power, date):
        for width in range(bands.shape[0]):
            for j in range(*span):
                (total,) = over_columns([power[date, :, j * BLOCK : (j + 2) * BLOCK]], width)
                own_box[date, width, :, j * BLOCK : (j + 1) * BLOCK] = total

    def pair(t, date, code):
        width = code % CODE - NARROW
        for stripe in near_stripes:
            u_re, u_im, ue_re, ue_im = own_stripe(date, stripe)
            v_re, v_im, ve_re, ve_im = other_stripe(t, stripe)
            over_rows(split, 0, stripe, 0, u_re * v_re + u_im * v_im, ue_re * ve_re + ue_im * ve_im)
            over_rows(split, 0, stripe, 1, u_im * v_re - u_re * v_im, ue_im * ve_re - ue_re * ve_im)
        for j in range(*span):
            at = slice(j * BLOCK, (j + 2) * BLOCK)
            re, im, power = over_columns([split[0, :, at], other_power[t, :, at]], width)
            square = re * re + im * im
            magnitude = square * lax.rsqrt(jnp.maximum(square, SMALLEST))
            value = magnitude * lax.rsqrt(own_box[date, width, :, j * BLOCK : (j + 1) * BLOCK] * power)
            results[t * dates_dev + date, :, j * BLOCK : (j + 1) * BLOCK] = value.astype(jnp.bfloat16)

    def copy_of(ref, at, date, slot, number):
        source, target = ref.at[at], out.at[date, slot]
        if ref is results and span != (0, cols // BLOCK):
            columns = slice(span[0] * BLOCK, span[1] * BLOCK)
            source, target = ref.at[at, :, columns], out.at[date, slot, :, columns]
        return pltpu.make_async_copy(source, target, sems.at[number + at])

    def copies_of(ref, rows_at, number):
        found = []
        for t, row in enumerate(rows_at):
            for date in range(dates_dev):
                code, at = codes[row, date], t * dates_dev + date
                found.append((code >= 0, copy_of(ref, at, date, jnp.maximum(code, 0) // CODE, number)))
        return found

    def zero_copies():
        found = []
        for date in range(dates_dev):
            held = [codes[row, date] // CODE for rows_at in (*places, rows_of, final_rows) for row in rows_at]
            for slot in range(out.shape[1]):
                empty = functools.reduce(jnp.logical_and, [code != slot for code in held])
                at = date * out.shape[1] + slot
                found.append((empty, pltpu.make_async_copy(zeros, out.at[date, slot], zero_sems.at[at])))
        return found

    def each(items, action):
        for condition, copy in items:

            @pl.when(condition)
            def _(copy=copy):
                getattr(copy, action)()

    pending, own_copies = [], []
    if role == "gather":
        zeros[...] = jnp.zeros_like(zeros)
        number = here * dates_dev
        for ref, rows_at in zip(earlier, places):
            pending += copies_of(ref, rows_at, number)
            number += len(rows_at) * dates_dev
        pending += zero_copies()
        each(pending, "start")
    if role in ("gather", "final"):
        own_copies = copies_of(results, rows_of, 0)
    if role == "first":
        for date in range(dates_dev):
            fill_power(other_power, date, own_stripe, date)
            fill_box(other_power, date)
    for t, row in enumerate(rows_of):
        found = [codes[row, date] for date in range(dates_dev)]

        @pl.when(functools.reduce(jnp.maximum, found) >= 0)
        def _(t=t, found=found):
            pad(split, 0)
            if role != "first":
                fill_power(other_power, t, other_stripe, t)

            def body(date, carry):
                code = found[0]
                for k in range(1, dates_dev):
                    code = jnp.where(date == k, found[k], code)

                @pl.when(code >= 0)
                def _():
                    pair(t, date, code)
                    if own_copies:
                        copy_of(results, t * dates_dev + date, date, code // CODE, 0).start()

                return carry

            lax.fori_loop(0, dates_dev, body, 0)

    each(pending + own_copies, "wait")


def stage(role, rows_of, tables, own, own_edge, other, layout, span, *state, places=(), final_rows=(), slots=None):
    dates_dev, _, rows, cols = own.shape
    here = len(rows_of)
    vmem, anywhere = pl.BlockSpec(memory_space=pltpu.VMEM), pl.BlockSpec(memory_space=pl.ANY)
    padded = cols + BLOCK
    span = span or (0, cols // BLOCK)
    results = (here * dates_dev, rows, cols)
    scratch = [pltpu.VMEM((2, rows + 2 * TOP, LANES), jnp.float32), pltpu.VMEM((1, 4 * rows, padded), jnp.bfloat16)]
    scratch.append(pltpu.VMEM((here, 2 * rows, padded), jnp.bfloat16))
    out_shape, out_specs = jax.ShapeDtypeStruct(results, jnp.bfloat16), vmem
    if role == "first":
        out_shape = (out_shape, jax.ShapeDtypeStruct((dates_dev, WIDE - NARROW + 1, rows, cols), jnp.float32))
        out_specs = (vmem, vmem)
    args = [*tables, own, own_edge, *other, *state]
    in_specs = [vmem] * len(args)
    aliases = {}
    if role in ("gather", "final"):
        out_shape, out_specs = jax.ShapeDtypeStruct((dates_dev, slots, rows, cols), jnp.bfloat16), anywhere
        count = here + sum(len(p) for p in places)
        scratch += [pltpu.VMEM(results, jnp.bfloat16), pltpu.SemaphoreType.DMA((count * dates_dev,))]
    if role == "gather":
        scratch += [pltpu.VMEM((rows, cols), jnp.bfloat16), pltpu.SemaphoreType.DMA((dates_dev * slots,))]
    if role == "final":
        in_specs[-1] = anywhere
        aliases = {len(args) - 1: 0}
    return pl.pallas_call(
        functools.partial(stage_kernel, role, rows_of, layout, span, places, final_rows, len(other)),
        out_shape=out_shape,
        in_specs=in_specs,
        out_specs=out_specs,
        scratch_shapes=scratch,
        input_output_aliases=aliases,
        compiler_params=pltpu.CompilerParams(vmem_limit_bytes=16 << 20),
        cost_estimate=pl.CostEstimate(flops=1 << 30, bytes_accessed=1 << 22, transcendentals=0),
    )(*args)


def gather_rows(part, own, pieces):
    rows = own.shape[2]
    for k, (date, plane, column) in enumerate(pieces):
        part[0, k * rows : (k + 1) * rows] = own[date, plane, :, column : column + part.shape[2]]


def prepare_kernel(pieces, own, edge, *parts):
    dates_dev, planes, rows, _ = own.shape
    upper = lax.axis_index("row") == 0
    for part, pieces_of in zip(parts, pieces):
        gather_rows(part, own, pieces_of)
    for date in range(dates_dev):
        for plane in range(planes):
            edge[date, plane] = jnp.where(upper, own[date, plane, rows - HALO :], own[date, plane, :HALO])


def prepare(own, pieces):
    dates_dev, planes, rows, cols = own.shape
    vmem = pl.BlockSpec(memory_space=pltpu.VMEM)
    shapes = [jax.ShapeDtypeStruct((dates_dev, planes, HALO, cols), own.dtype)]
    shapes += [jax.ShapeDtypeStruct((1, len(p) * rows, width), own.dtype) for p, width in pieces]
    return pl.pallas_call(
        functools.partial(prepare_kernel, [p for p, _ in pieces]),
        out_shape=shapes,
        in_specs=[vmem],
        out_specs=[vmem] * len(shapes),
        name="prepare",
        compiler_params=pltpu.CompilerParams(vmem_limit_bytes=16 << 20),
    )(own)


def table_kernel(total_dates, dates_dev, partners, counts, windows, table, partners_at, counts_at, windows_at, sems):
    pairs = ((partners, partners_at), (counts, counts_at), (windows, windows_at))
    copies = [pltpu.make_async_copy(source, target, sems.at[k]) for k, (source, target) in enumerate(pairs)]
    for copy in copies:
        copy.start()
    for copy in copies:
        copy.wait()
    first_date = lax.axis_index("date") * dates_dev
    row, column = (lax.broadcasted_iota(jnp.int32, table.shape, k) for k in range(2))
    found = jnp.full(table.shape, -1, jnp.int32)
    for date in range(dates_dev):
        for slot in range(partners.shape[1]):
            ahead = partners_at[date, slot] - first_date
            ahead = jnp.where(ahead < 0, ahead + total_dates, ahead)
            code = jnp.where(slot < counts_at[date], slot * CODE + windows_at[date, slot], -1)
            here = jnp.logical_and(row == ahead, column == date)
            found = jnp.maximum(found, jnp.where(here, code, -1))
    table[...] = found


def table_of(partners, counts, windows, total_dates, reached):
    anywhere = pl.BlockSpec(memory_space=pl.ANY)
    return pl.pallas_call(
        functools.partial(table_kernel, total_dates, partners.shape[0]),
        out_shape=jax.ShapeDtypeStruct((reached, partners.shape[0]), jnp.int32),
        in_specs=[anywhere] * 3,
        out_specs=pl.BlockSpec(memory_space=pltpu.VMEM),
        scratch_shapes=[pltpu.SMEM(x.shape, x.dtype) for x in (partners, counts, windows)]
        + [pltpu.SemaphoreType.DMA((3,))],
        name="table",
        compiler_params=pltpu.CompilerParams(vmem_limit_bytes=1 << 20),
    )(partners, counts, windows)


def attach_kernel(pieces, own, own_edge, part):
    dates_dev, planes, rows, _ = own.shape
    gather_rows(part, own, pieces)
    for date in range(dates_dev):
        for plane in range(planes):
            start = len(pieces) * rows + (planes * date + plane) * HALO
            part[0, start : start + HALO] = own_edge[date, plane]


def attach(own, own_edge, pieces):
    dates_dev, planes, rows, cols = own.shape
    vmem = pl.BlockSpec(memory_space=pltpu.VMEM)
    return pl.pallas_call(
        functools.partial(attach_kernel, pieces),
        out_shape=jax.ShapeDtypeStruct((1, len(pieces) * rows + dates_dev * planes * HALO, cols), own.dtype),
        in_specs=[vmem] * 2,
        out_specs=vmem,
        name="attach",
        compiler_params=pltpu.CompilerParams(vmem_limit_bytes=16 << 20),
    )(own, own_edge)


def relayed(own, loop_size, edge_move):
    rows = own.shape[2]
    by_two = [((i + 2) % loop_size, i) for i in range(loop_size)]
    by_one = [((i + 1) % loop_size, i) for i in range(loop_size)]
    within = [(i + 1 - 2 * (i % 2), i) for i in range(loop_size)]
    is_odd = lax.rem(lax.axis_index("date"), 2) == 1
    cols = own.shape[3]
    edge, first, far_part = prepare(own, ((((0, 0, 0), (0, 1, 0)), cols), (((1, 0, 0), (1, 1, 0)), cols)))
    own_edge = edge_move(edge, 0)
    near_part = attach(own, own_edge, ((1, 0, 0), (1, 1, 0)))
    far_first = lax.ppermute(first, "date", by_two)
    near_second = lax.ppermute(near_part, "date", by_one)
    far_edge = edge_move(edge, 2)
    far_second = lax.ppermute(far_part, "date", by_two)
    chosen = jnp.where(is_odd, first, far_first)
    near_first = lax.ppermute(chosen, "date", within)

    def whole_edges(date):
        return lambda stripe: ((0, 0, 0), (0, rows, 0), (1, date, 0), (1, date, 1))

    return own_edge, [
        ((4,), [far_first, far_edge], whole_edges(0), None),
        ((3,), [near_second], lambda stripe: ((0, 0, 0), (0, rows, 0), (0, 2 * rows + 2 * HALO, 0), (0, 2 * rows + 3 * HALO, 0)), None),
        ((2,), [near_first, near_second], lambda stripe: ((0, 0, 0), (0, rows, 0), (1, 2 * rows, 0), (1, 2 * rows + HALO, 0)), None),
        ((5,), [far_second, far_edge], whole_edges(1), None),
    ]


def whole(slc_stack, partners, counts, windows):
    dates_dev, _, _, _ = slc_stack.shape
    per_date = partners.shape[1]
    loop_size = lax.axis_size("date")
    strips = lax.axis_size("row")
    assert strips == 2
    reach = loop_size // 4
    total_dates = dates_dev * loop_size
    reached = (reach + 1) * dates_dev
    tables = (table_of(partners, counts, windows, total_dates, reached), band_table())

    def edge_move(edge, distance):
        pairs = [
            (((i + distance) % loop_size) * strips + (1 - r), i * strips + r) for i in range(loop_size) for r in range(strips)
        ]
        return lax.ppermute(edge, ("date", "row"), pairs)

    if reach == 2 and dates_dev == 2:
        own_edge, arrivals = relayed(slc_stack, loop_size, edge_move)
    else:
        (edge,) = prepare(slc_stack, ())
        own_edge, arrivals = edge_move(edge, 0), []
        for distance in range(1, reach + 1):
            block = lax.ppermute(slc_stack, "date", [((i + distance) % loop_size, i) for i in range(loop_size)])
            rows_of = tuple(range(distance * dates_dev, (distance + 1) * dates_dev))
            arrivals.append((rows_of, [block, edge_move(edge, distance)], None, None))
    places = [tuple(range(dates_dev))]
    own = (tables, slc_stack, own_edge)
    result, own_box = stage("first", places[0], *own, [slc_stack, own_edge], None, None)
    results = [result]
    for number, (rows_of, *block) in enumerate(arrivals):
        left = len(arrivals) - number
        if left > 2:
            results.append(stage("middle", rows_of, *own, *block, own_box))
            places.append(rows_of)
        elif left == 2:
            known = {"places": tuple(places), "final_rows": arrivals[-1][0], "slots": per_date}
            out = stage("gather", rows_of, *own, *block, own_box, *results, **known)
        else:
            out = stage("final", rows_of, *own, *block, own_box, out, slots=per_date)
    return out


def solution(mesh):
    in_specs = (
        P("date", None, ("tiles", "row"), None),
        P("date", None),
        P("date"),
        P("date", None),
    )
    out_specs = P("date", None, ("tiles", "row"), None)
    return jax.shard_map(whole, mesh=mesh, in_specs=in_specs, out_specs=out_specs, check_vma=False)
```

time: 150 us -> 34.7 us (0.23)
  loops' own time: 41.1 us -> 0 us
  starting transfers between devices: 37 us -> 8.22 us
  other arithmetic: 27.6 us -> 0.3 us
  local copies, waits for them, and re-layouts: 25.7 us -> 3.05 us
  Pallas kernels: 0 us -> 6.83 us
    another operation x1 -> x0, loops' own time: 41.1 us -> none  [run_items(): lax.scan(compute, jnp.int32(0), (own_index[ordering], flat_partners[order...]
    ppermute x14 -> x6, starting transfers between devices: 37 us -> 8.22 us  [the longest x2 5.25 us: edge_move(): return lax.ppermute(edge, ('date', 'row'), pairs)]
    add x19 -> x1, other arithmetic: 20.4 us -> 0.01 us  [band_table(): width = lax.broadcasted_iota(jnp.int32, shape, 0) + NARROW]
    dynamic_slice x24 -> x0, local copies, waits for them, and re-layouts: 18.8 us -> none  [run_items(): lax.scan(compute, jnp.int32(0), (own_index[ordering], flat_partners[order...]
    pallas_call x0 -> x8, Pallas kernels: none -> 6.83 us  [the longest x5 6.14 us: stage(): pl.pallas_call(functools.partial(stage_kernel, role, rows_of, layout, spa...]
    dynamic_update_slice x6 -> x0, other arithmetic: 4.6 us -> none  [run_items(): lax.scan(compute, jnp.int32(0), (own_index[ordering], flat_partners[order...]
    gather x4 -> x0, local copies, waits for them, and re-layouts: 3.16 us -> none  [the longest x1 1.22 us: run_items(): flat_partners[ordering]]
    unnamed x6 -> x10, local copies, waits for them, and re-layouts: 0.97 us -> 3.05 us
  transfers between devices with their start and end apart: 14 -> 6, of which waited for: 8 -> 3; matrix products, arithmetic and copies ran while one was open for 6% -> 1% of each run, Pallas kernels for 0% -> 15%
where the time goes in v3:
time: 34.7 us; the launch traced here: 34.5 us
  waiting for transfers between devices  15.9 us (46%)
  starting transfers between devices  8.22 us (24%)
  Pallas kernels  6.83 us (20%)
  local copies, waits for them, and re-layouts  3.05 us (9%)
    ppermute x1, waiting for transfers between devices, relayed(): far_first = lax.ppermute(first, 'date', by_two)  9.45 us
    ppermute x1, waiting for transfers between devices, relayed(): near_first = lax.ppermute(chosen, 'date', within)  6.33 us
    pallas_call x5, Pallas kernels, stage(): pl.pallas_call(functools.partial(stage_kernel, role, rows_of, layout, spa...  6.14 us
    ppermute x2, starting transfers between devices, edge_move(): return lax.ppermute(edge, ('date', 'row'), pairs)  5.25 us
    unnamed x10, local copies, waits for them, and re-layouts  3.05 us
    ppermute x1, starting transfers between devices, relayed(): near_second = lax.ppermute(near_part, 'date', by_one)  1.46 us
  transfers between devices with their start and end apart: 6, of which 3 were waited for; matrix products, arithmetic and copies ran while one was open for 1% of the time, Pallas kernels for 15%

profile of v3, /device:TPU:0, one launch (start us, length us, event | category | flops | bytes accessed | tf_op | source)
XLA Modules:
  0.0 34.5 jit_solution(12077829658036706737)
XLA Ops:
  0.0 1.0 %copy-done = bf16[2,2,64,1024]{3,2,1,0:T(8,128)(2,1)S(1)} copy-done((bf16[2,2,64,1024]{3,2,1,0:T(8,128)(2,1)S(1)}, bf16[2,2,64,1024]{3,2,1,0:T(8,128)(2,1)}, u32[]{:S(2)}) %copy-start) | copy-done | bytes 524312
  1.1 4.6 %collective-permute-start.2 = (bf16[2,2,2,1024]{3,2,1,0:T(2,128)(2,1)S(1)}, bf16[2,2,2,1024]{3,2,1,0:T(2,128)(2,1)S(1)}, u32[]{:S(2)}, u32[]{:S(2)}) collective-permute-start(bf16[2,2,2,1024]{3,2,1,0:T(2,128)(2,1)S(1)} %get-tuple-element.10), channel_id=1, source_target_pairs={{5,0},{4,1},{7,2},{6,3},{9,4},{8,5},{11,6},{10,7},{13,8},{12,9},{1... | collective-permute-start | bytes 49160 | tf_op jit(solution)/shard_map/ppermute | solution.py:359
  5.7 0.7 %collective-permute-start = (bf16[2,2,2,1024]{3,2,1,0:T(2,128)(2,1)S(1)}, bf16[2,2,2,1024]{3,2,1,0:T(2,128)(2,1)S(1)}, u32[]{:S(2)}, u32[]{:S(2)}) collective-permute-start(bf16[2,2,2,1024]{3,2,1,0:T(2,128)(2,1)S(1)} %get-tuple-element.10), channel_id=1, source_target_pairs={{1,0},{0,1},{3,2},{2,3},{5,4},{4,5},{7,6},{6,7},{9,8},{8,9},{11,10... | collective-permute-start | bytes 49160 | tf_op jit(solution)/shard_map/ppermute | solution.py:359
  6.3 0.4 %collective-permute-start.1 = (bf16[1,128,1024]{2,1,0:T(8,128)(2,1)S(1)}, bf16[1,128,1024]{2,1,0:T(8,128)(2,1)S(1)}, u32[]{:S(2)}, u32[]{:S(2)}) collective-permute-start(bf16[1,128,1024]{2,1,0:T(8,128)(2,1)S(1)} %get-tuple-element.11), channel_id=1, source_target_pairs={{4,0},{6,2},{8,4},{10,6},{12,8},{14,10},{0,12},{2,14},{5,1},{7,3},... | collective-permute-start | bytes 786440 | tf_op jit(solution)/shard_map/ppermute | solution.py:329
  6.8 0.4 %collective-permute-start.3 = (bf16[1,128,1024]{2,1,0:T(8,128)(2,1)S(1)}, bf16[1,128,1024]{2,1,0:T(8,128)(2,1)S(1)}, u32[]{:S(2)}, u32[]{:S(2)}) collective-permute-start(bf16[1,128,1024]{2,1,0:T(8,128)(2,1)S(1)} %get-tuple-element.13), channel_id=1, source_target_pairs={{4,0},{6,2},{8,4},{10,6},{12,8},{14,10},{0,12},{2,14},{5,1},{7,3},... | collective-permute-start | bytes 786440 | tf_op jit(solution)/shard_map/ppermute | solution.py:326
  7.2 0.3 select_convert_fusion.refs_1_
  7.5 0.0 copy-start.2
  7.5 0.7 %copy-done.2 = s32[2,4]{1,0:T(2,128)S(1)} copy-done((s32[2,4]{1,0:T(2,128)S(1)}, s32[2,4]{1,0:T(2,128)}, u32[]{:S(2)}) %copy-start.2) | copy-done | bytes 56
  8.2 0.7 %copy-done.3 = s32[2,4]{1,0:T(2,128)S(1)} copy-done((s32[2,4]{1,0:T(2,128)S(1)}, s32[2,4]{1,0:T(2,128)}, u32[]{:S(2)}) %copy-start.3) | copy-done | bytes 56
  8.9 0.7 %copy-done.4 = s32[2]{0:T(128)S(1)} copy-done((s32[2]{0:T(128)S(1)}, s32[2]{0:T(128)}, u32[]{:S(2)}) %copy-start.4) | copy-done | bytes 32
  9.5 0.6 %table.1.refs_0_ = s32[6,2]{1,0:T(8,128)S(1)} custom-call(s32[2,4]{1,0:T(2,128)S(1)} %copy-done.2, s32[2]{0:T(128)S(1)} %copy-done.4, s32[2,4]{1,0:T(2,128)S(1)} %copy-done.3), custom_call_target="tpu_custom_call" | custom-call | tf_op jit(solution)/shard_map/table/pallas_call | solution.py:282
  10.2 0.0 collective-permute-done.refs_3_.refs_5_.own_edge
  10.2 1.5 %collective-permute-start.5 = (bf16[1,136,1024]{2,1,0:T(8,128)(2,1)S(1)}, bf16[1,136,1024]{2,1,0:T(8,128)(2,1)S(1)}, u32[]{:S(2)}, u32[]{:S(2)}) collective-permute-start(bf16[1,136,1024]{2,1,0:T(8,128)(2,1)S(1)} %attach.1), channel_id=1, source_target_pairs={{2,0},{4,2},{6,4},{8,6},{10,8},{12,10},{14,12},{0,14},{3,1},{5,3},... | collective-permute-start | bytes 835592 | tf_op jit(solution)/shard_map/ppermute | solution.py:327
  11.7 9.5 %collective-permute-done.3.refs_4_ = bf16[1,128,1024]{2,1,0:T(8,128)(2,1)S(1)} collective-permute-done((bf16[1,128,1024]{2,1,0:T(8,128)(2,1)S(1)}, bf16[1,128,1024]{2,1,0:T(8,128)(2,1)S(1)}, u32[]{:S(2)}, u32[]{:S(2)}) %collective-permute-start.3) | collective-permute-done | bytes 262176 | tf_op jit(solution)/shard_map/ppermute | solution.py:326
  21.2 0.6 %collective-permute-start.4 = (bf16[1,128,1024]{2,1,0:T(8,128)(2,1)S(1)}, bf16[1,128,1024]{2,1,0:T(8,128)(2,1)S(1)}, u32[]{:S(2)}, u32[]{:S(2)}) collective-permute-start(bf16[1,128,1024]{2,1,0:T(8,128)(2,1)S(1)} %broadcast_select_fusion), channel_id=1, source_target_pairs={{2,0},{0,2},{6,4},{4,6},{10,8},{8,10},{14,12},{12,14},{3,1},{1,3},... | collective-permute-start | bytes 786440 | tf_op jit(solution)/shard_map/ppermute | solution.py:331
  21.8 1.3 %shard_map.46 = (bf16[4,64,1024]{2,1,0:T(8,128)(2,1)S(1)}, f32[2,3,64,1024]{3,2,1,0:T(8,128)S(1)}) custom-call(s32[6,2]{1,0:T(8,128)S(1)} %table.1.refs_0_, bf16[3,512,256]{2,1,0:T(8,128)(2,1)S(1)} %select_convert_fusion.refs_1_, bf16[2,2,64,1024]{3,2,1,0:T(8,128)(2,1)S(1)} %copy-done.1, ...), custom_call_target="tpu_custom_call" | custom-call | flops 1073741824 | bytes 4194304 | tf_op jit(solution)/shard_map/pallas_call | solution.py:217
  23.1 0.0 collective-permute-done.2.refs_5_
  23.1 1.0 %shard_map.47.refs_8_ = bf16[2,64,1024]{2,1,0:T(8,128)(2,1)S(1)} custom-call(s32[6,2]{1,0:T(8,128)S(1)} %table.1.refs_0_, bf16[3,512,256]{2,1,0:T(8,128)(2,1)S(1)} %select_convert_fusion.refs_1_, bf16[2,2,64,1024]{3,2,1,0:T(8,128)(2,1)S(1)} %copy-done.1, bf16[2,2,2,1024]{3,2,1,0:T(2,128)(2,1)S(1)} %collective-permute-done.refs_3_.refs_5_.own_edge, ...), custom_call_target="tpu_custom_call" | custom-call | flops 1073741824 | bytes 4194304 | tf_op jit(solution)/shard_map/pallas_call | solution.py:217
  24.1 0.1 collective-permute-done.5.refs_4_.refs_5_
  24.3 0.1 shard_map.48.refs_9_
  24.4 6.3 %collective-permute-done.4.refs_4_ = bf16[1,128,1024]{2,1,0:T(8,128)(2,1)S(1)} collective-permute-done((bf16[1,128,1024]{2,1,0:T(8,128)(2,1)S(1)}, bf16[1,128,1024]{2,1,0:T(8,128)(2,1)S(1)}, u32[]{:S(2)}, u32[]{:S(2)}) %collective-permute-start.4) | collective-permute-done | bytes 262176 | tf_op jit(solution)/shard_map/ppermute | solution.py:331
  30.7 2.0 %shard_map.49.refs_7_ = bf16[2,4,64,1024]{3,2,1,0:T(8,128)(2,1)} custom-call(s32[6,2]{1,0:T(8,128)S(1)} %table.1.refs_0_, bf16[3,512,256]{2,1,0:T(8,128)(2,1)S(1)} %select_convert_fusion.refs_1_, bf16[2,2,64,1024]{3,2,1,0:T(8,128)(2,1)S(1)} %copy-done.1, bf16[2,2,2,1024]{3,2,1,0:T(2,128)(2,1)S(1)} %collective-permute-done.refs_3_.refs_5_.own_edge, ...), custom_call_target="tpu_custom_call" | custom-call | flops 1073741824 | bytes 4194304 | tf_op jit(solution)/shard_map/pallas_call | solution.py:217
  32.7 0.0 collective-permute-done.1.refs_4_
  32.8 1.7 %shard_map.50 = bf16[2,4,64,1024]{3,2,1,0:T(8,128)(2,1)} custom-call(s32[6,2]{1,0:T(8,128)S(1)} %table.1.refs_0_, bf16[3,512,256]{2,1,0:T(8,128)(2,1)S(1)} %select_convert_fusion.refs_1_, bf16[2,2,64,1024]{3,2,1,0:T(8,128)(2,1)S(1)} %copy-done.1, ...), custom_call_target="tpu_custom_call", output_to_operand_aliasing={{}: (7, {})} | custom-call | flops 1073741824 | bytes 4194304 | tf_op jit(solution)/shard_map/pallas_call | solution.py:217
  (10 shorter events, 0.1 us)
Async XLA Ops:
  0.0 1.0 %copy-start = (bf16[2,2,64,1024]{3,2,1,0:T(8,128)(2,1)S(1)}, bf16[2,2,64,1024]{3,2,1,0:T(8,128)(2,1)}, u32[]{:S(2)}) copy-start(bf16[2,2,64,1024]{3,2,1,0:T(8,128)(2,1)} %refs_2_.9) | copy-start | bytes 1572868
  1.0 9.1 %copy-start.1 = (bf16[2,2,64,1024]{3,2,1,0:T(8,128)(2,1)S(1)}, bf16[2,2,64,1024]{3,2,1,0:T(8,128)(2,1)}, u32[]{:S(2)}) copy-start(bf16[2,2,64,1024]{3,2,1,0:T(8,128)(2,1)} %refs_2_.9) | copy-start | bytes 1572868
  1.1 22.0 %collective-permute-start.2 = (bf16[2,2,2,1024]{3,2,1,0:T(2,128)(2,1)S(1)}, bf16[2,2,2,1024]{3,2,1,0:T(2,128)(2,1)S(1)}, u32[]{:S(2)}, u32[]{:S(2)}) collective-permute-start(bf16[2,2,2,1024]{3,2,1,0:T(2,128)(2,1)S(1)} %get-tuple-element.10), channel_id=1, source_target_pairs={{5,0},{4,1},{7,2},{6,3},{9,4},{8,5},{11,6},{10,7},{13,8},{12,9},{1... | collective-permute-start | bytes 49160 | tf_op jit(solution)/shard_map/ppermute | solution.py:359
  5.7 4.5 %collective-permute-start = (bf16[2,2,2,1024]{3,2,1,0:T(2,128)(2,1)S(1)}, bf16[2,2,2,1024]{3,2,1,0:T(2,128)(2,1)S(1)}, u32[]{:S(2)}, u32[]{:S(2)}) collective-permute-start(bf16[2,2,2,1024]{3,2,1,0:T(2,128)(2,1)S(1)} %get-tuple-element.10), channel_id=1, source_target_pairs={{1,0},{0,1},{3,2},{2,3},{5,4},{4,5},{7,6},{6,7},{9,8},{8,9},{11,10... | collective-permute-start | bytes 49160 | tf_op jit(solution)/shard_map/ppermute | solution.py:359
  6.3 26.4 %collective-permute-start.1 = (bf16[1,128,1024]{2,1,0:T(8,128)(2,1)S(1)}, bf16[1,128,1024]{2,1,0:T(8,128)(2,1)S(1)}, u32[]{:S(2)}, u32[]{:S(2)}) collective-permute-start(bf16[1,128,1024]{2,1,0:T(8,128)(2,1)S(1)} %get-tuple-element.11), channel_id=1, source_target_pairs={{4,0},{6,2},{8,4},{10,6},{12,8},{14,10},{0,12},{2,14},{5,1},{7,3},... | collective-permute-start | bytes 786440 | tf_op jit(solution)/shard_map/ppermute | solution.py:329
  6.8 14.3 %collective-permute-start.3 = (bf16[1,128,1024]{2,1,0:T(8,128)(2,1)S(1)}, bf16[1,128,1024]{2,1,0:T(8,128)(2,1)S(1)}, u32[]{:S(2)}, u32[]{:S(2)}) collective-permute-start(bf16[1,128,1024]{2,1,0:T(8,128)(2,1)S(1)} %get-tuple-element.13), channel_id=1, source_target_pairs={{4,0},{6,2},{8,4},{10,6},{12,8},{14,10},{0,12},{2,14},{5,1},{7,3},... | collective-permute-start | bytes 786440 | tf_op jit(solution)/shard_map/ppermute | solution.py:326
  7.5 0.7 %copy-start.2 = (s32[2,4]{1,0:T(2,128)S(1)}, s32[2,4]{1,0:T(2,128)}, u32[]{:S(2)}) copy-start(s32[2,4]{1,0:T(2,128)} %partners.1) | copy-start | bytes 100
  8.2 0.7 %copy-start.3 = (s32[2,4]{1,0:T(2,128)S(1)}, s32[2,4]{1,0:T(2,128)}, u32[]{:S(2)}) copy-start(s32[2,4]{1,0:T(2,128)} %windows.1) | copy-start | bytes 100
  8.9 0.7 %copy-start.4 = (s32[2]{0:T(128)S(1)}, s32[2]{0:T(128)}, u32[]{:S(2)}) copy-start(s32[2]{0:T(128)} %counts.1) | copy-start | bytes 28
  10.2 14.1 %collective-permute-start.5 = (bf16[1,136,1024]{2,1,0:T(8,128)(2,1)S(1)}, bf16[1,136,1024]{2,1,0:T(8,128)(2,1)S(1)}, u32[]{:S(2)}, u32[]{:S(2)}) collective-permute-start(bf16[1,136,1024]{2,1,0:T(8,128)(2,1)S(1)} %attach.1), channel_id=1, source_target_pairs={{2,0},{4,2},{6,4},{8,6},{10,8},{12,10},{14,12},{0,14},{3,1},{5,3},... | collective-permute-start | bytes 835592 | tf_op jit(solution)/shard_map/ppermute | solution.py:327
  21.2 9.6 %collective-permute-start.4 = (bf16[1,128,1024]{2,1,0:T(8,128)(2,1)S(1)}, bf16[1,128,1024]{2,1,0:T(8,128)(2,1)S(1)}, u32[]{:S(2)}, u32[]{:S(2)}) collective-permute-start(bf16[1,128,1024]{2,1,0:T(8,128)(2,1)S(1)} %broadcast_select_fusion), channel_id=1, source_target_pairs={{2,0},{0,2},{6,4},{4,6},{10,8},{8,10},{14,12},{12,14},{3,1},{1,3},... | collective-permute-start | bytes 786440 | tf_op jit(solution)/shard_map/ppermute | solution.py:331

commit v4 on v3

--- a/solution.py
+++ b/solution.py
@@ -43,7 +43,9 @@
         earlier, refs = refs[: len(places)], refs[len(places) :]
         out, products, split, other_power, results, sems, zeros, zero_sems = refs
     else:
-        own_box, _, out, products, split, other_power, results, sems = refs
+        own_box, *refs = refs
+        earlier, refs = refs[: len(places)], refs[len(places) :]
+        _, out, products, split, other_power, results, sems = refs
     codes = table[...]
 
     def pad(ref, at):
@@ -133,7 +135,7 @@
     def zero_copies():
         found = []
         for date in range(dates_dev):
-            held = [codes[row, date] // CODE for rows_at in (*places, rows_of, final_rows) for row in rows_at]
+            held = [codes[row, date] // CODE for rows_at in (*places, rows_of, *final_rows) for row in rows_at]
             for slot in range(out.shape[1]):
                 empty = functools.reduce(jnp.logical_and, [code != slot for code in held])
                 at = date * out.shape[1] + slot
@@ -148,15 +150,15 @@
                 getattr(copy, action)()
 
     pending, own_copies = [], []
-    if role == "gather":
-        zeros[...] = jnp.zeros_like(zeros)
+    if role in ("gather", "final"):
         number = here * dates_dev
         for ref, rows_at in zip(earlier, places):
             pending += copies_of(ref, rows_at, number)
             number += len(rows_at) * dates_dev
-        pending += zero_copies()
+        if role == "gather":
+            zeros[...] = jnp.zeros_like(zeros)
+            pending += zero_copies()
         each(pending, "start")
-    if role in ("gather", "final"):
         own_copies = copies_of(results, rows_of, 0)
     if role == "first":
         for date in range(dates_dev):
@@ -373,14 +375,15 @@
     results = [result]
     for number, (rows_of, *block) in enumerate(arrivals):
         left = len(arrivals) - number
-        if left > 2:
+        if left == 3:
+            known = {"places": tuple(places), "final_rows": tuple(a[0] for a in arrivals[-2:]), "slots": per_date}
+            out = stage("gather", rows_of, *own, *block, own_box, *results, **known)
+            places, results = [], []
+        elif left == 1:
+            out = stage("final", rows_of, *own, *block, own_box, *results, out, places=tuple(places), slots=per_date)
+        else:
             results.append(stage("middle", rows_of, *own, *block, own_box))
             places.append(rows_of)
-        elif left == 2:
-            known = {"places": tuple(places), "final_rows": arrivals[-1][0], "slots": per_date}
-            out = stage("gather", rows_of, *own, *block, own_box, *results, **known)
-        else:
-            out = stage("final", rows_of, *own, *block, own_box, out, slots=per_date)
     return out
 
 

time: 34.7 us -> 33.7 us (0.971)
  waiting for transfers between devices: 15.9 us -> 14.9 us
    ppermute x1, waiting for transfers between devices: 6.33 us -> 5.25 us  [relayed(): near_first = lax.ppermute(chosen, 'date', within)]
  transfers between devices with their start and end apart: 6 -> 6, of which waited for: 3 -> 3; matrix products, arithmetic and copies ran while one was open for 1% -> 1% of each run, Pallas kernels for 15% -> 16%
where the time goes in v4:
time: 33.7 us; the launch traced here: 33.5 us
  waiting for transfers between devices  14.9 us (44%)
  starting transfers between devices  8.22 us (24%)
  Pallas kernels  6.99 us (21%)
  local copies, waits for them, and re-layouts  3.05 us (9%)
    ppermute x1, waiting for transfers between devices, relayed(): far_first = lax.ppermute(first, 'date', by_two)  9.45 us
    pallas_call x5, Pallas kernels, stage(): pl.pallas_call(functools.partial(stage_kernel, role, rows_of, layout, spa...  6.29 us
    ppermute x1, waiting for transfers between devices, relayed(): near_first = lax.ppermute(chosen, 'date', within)  5.25 us
    ppermute x2, starting transfers between devices, edge_move(): return lax.ppermute(edge, ('date', 'row'), pairs)  5.25 us
    unnamed x10, local copies, waits for them, and re-layouts  3.05 us
    ppermute x1, starting transfers between devices, relayed(): near_second = lax.ppermute(near_part, 'date', by_one)  1.46 us
  transfers between devices with their start and end apart: 6, of which 3 were waited for; matrix products, arithmetic and copies ran while one was open for 1% of the time, Pallas kernels for 16%

profile of v4, /device:TPU:0, one launch (start us, length us, event | category | flops | bytes accessed | tf_op | source)
XLA Modules:
  0.0 33.5 jit_solution(14604567406008566383)
XLA Ops:
  0.0 1.0 %copy-done = bf16[2,2,64,1024]{3,2,1,0:T(8,128)(2,1)S(1)} copy-done((bf16[2,2,64,1024]{3,2,1,0:T(8,128)(2,1)S(1)}, bf16[2,2,64,1024]{3,2,1,0:T(8,128)(2,1)}, u32[]{:S(2)}) %copy-start) | copy-done | bytes 524312
  1.1 4.6 %collective-permute-start.2 = (bf16[2,2,2,1024]{3,2,1,0:T(2,128)(2,1)S(1)}, bf16[2,2,2,1024]{3,2,1,0:T(2,128)(2,1)S(1)}, u32[]{:S(2)}, u32[]{:S(2)}) collective-permute-start(bf16[2,2,2,1024]{3,2,1,0:T(2,128)(2,1)S(1)} %get-tuple-element.10), channel_id=1, source_target_pairs={{5,0},{4,1},{7,2},{6,3},{9,4},{8,5},{11,6},{10,7},{13,8},{12,9},{1... | collective-permute-start | bytes 49160 | tf_op jit(solution)/shard_map/ppermute | solution.py:361
  5.7 0.7 %collective-permute-start = (bf16[2,2,2,1024]{3,2,1,0:T(2,128)(2,1)S(1)}, bf16[2,2,2,1024]{3,2,1,0:T(2,128)(2,1)S(1)}, u32[]{:S(2)}, u32[]{:S(2)}) collective-permute-start(bf16[2,2,2,1024]{3,2,1,0:T(2,128)(2,1)S(1)} %get-tuple-element.10), channel_id=1, source_target_pairs={{1,0},{0,1},{3,2},{2,3},{5,4},{4,5},{7,6},{6,7},{9,8},{8,9},{11,10... | collective-permute-start | bytes 49160 | tf_op jit(solution)/shard_map/ppermute | solution.py:361
  6.3 0.4 %collective-permute-start.1 = (bf16[1,128,1024]{2,1,0:T(8,128)(2,1)S(1)}, bf16[1,128,1024]{2,1,0:T(8,128)(2,1)S(1)}, u32[]{:S(2)}, u32[]{:S(2)}) collective-permute-start(bf16[1,128,1024]{2,1,0:T(8,128)(2,1)S(1)} %get-tuple-element.11), channel_id=1, source_target_pairs={{4,0},{6,2},{8,4},{10,6},{12,8},{14,10},{0,12},{2,14},{5,1},{7,3},... | collective-permute-start | bytes 786440 | tf_op jit(solution)/shard_map/ppermute | solution.py:331
  6.8 0.4 %collective-permute-start.3 = (bf16[1,128,1024]{2,1,0:T(8,128)(2,1)S(1)}, bf16[1,128,1024]{2,1,0:T(8,128)(2,1)S(1)}, u32[]{:S(2)}, u32[]{:S(2)}) collective-permute-start(bf16[1,128,1024]{2,1,0:T(8,128)(2,1)S(1)} %get-tuple-element.13), channel_id=1, source_target_pairs={{4,0},{6,2},{8,4},{10,6},{12,8},{14,10},{0,12},{2,14},{5,1},{7,3},... | collective-permute-start | bytes 786440 | tf_op jit(solution)/shard_map/ppermute | solution.py:328
  7.2 0.3 select_convert_fusion.refs_1_
  7.5 0.0 copy-start.2
  7.5 0.7 %copy-done.2 = s32[2,4]{1,0:T(2,128)S(1)} copy-done((s32[2,4]{1,0:T(2,128)S(1)}, s32[2,4]{1,0:T(2,128)}, u32[]{:S(2)}) %copy-start.2) | copy-done | bytes 56
  8.2 0.7 %copy-done.3 = s32[2,4]{1,0:T(2,128)S(1)} copy-done((s32[2,4]{1,0:T(2,128)S(1)}, s32[2,4]{1,0:T(2,128)}, u32[]{:S(2)}) %copy-start.3) | copy-done | bytes 56
  8.9 0.7 %copy-done.4 = s32[2]{0:T(128)S(1)} copy-done((s32[2]{0:T(128)S(1)}, s32[2]{0:T(128)}, u32[]{:S(2)}) %copy-start.4) | copy-done | bytes 32
  9.5 0.6 %table.1.refs_0_ = s32[6,2]{1,0:T(8,128)S(1)} custom-call(s32[2,4]{1,0:T(2,128)S(1)} %copy-done.2, s32[2]{0:T(128)S(1)} %copy-done.4, s32[2,4]{1,0:T(2,128)S(1)} %copy-done.3), custom_call_target="tpu_custom_call" | custom-call | tf_op jit(solution)/shard_map/table/pallas_call | solution.py:284
  10.2 0.0 collective-permute-done.refs_3_.refs_5_.own_edge
  10.2 1.5 %collective-permute-start.5 = (bf16[1,136,1024]{2,1,0:T(8,128)(2,1)S(1)}, bf16[1,136,1024]{2,1,0:T(8,128)(2,1)S(1)}, u32[]{:S(2)}, u32[]{:S(2)}) collective-permute-start(bf16[1,136,1024]{2,1,0:T(8,128)(2,1)S(1)} %attach.1), channel_id=1, source_target_pairs={{2,0},{4,2},{6,4},{8,6},{10,8},{12,10},{14,12},{0,14},{3,1},{5,3},... | collective-permute-start | bytes 835592 | tf_op jit(solution)/shard_map/ppermute | solution.py:329
  11.7 9.5 %collective-permute-done.3.refs_4_ = bf16[1,128,1024]{2,1,0:T(8,128)(2,1)S(1)} collective-permute-done((bf16[1,128,1024]{2,1,0:T(8,128)(2,1)S(1)}, bf16[1,128,1024]{2,1,0:T(8,128)(2,1)S(1)}, u32[]{:S(2)}, u32[]{:S(2)}) %collective-permute-start.3) | collective-permute-done | bytes 262176 | tf_op jit(solution)/shard_map/ppermute | solution.py:328
  21.2 0.6 %collective-permute-start.4 = (bf16[1,128,1024]{2,1,0:T(8,128)(2,1)S(1)}, bf16[1,128,1024]{2,1,0:T(8,128)(2,1)S(1)}, u32[]{:S(2)}, u32[]{:S(2)}) collective-permute-start(bf16[1,128,1024]{2,1,0:T(8,128)(2,1)S(1)} %broadcast_select_fusion), channel_id=1, source_target_pairs={{2,0},{0,2},{6,4},{4,6},{10,8},{8,10},{14,12},{12,14},{3,1},{1,3},... | collective-permute-start | bytes 786440 | tf_op jit(solution)/shard_map/ppermute | solution.py:333
  21.8 1.3 %shard_map.46 = (bf16[4,64,1024]{2,1,0:T(8,128)(2,1)S(1)}, f32[2,3,64,1024]{3,2,1,0:T(8,128)S(1)}) custom-call(s32[6,2]{1,0:T(8,128)S(1)} %table.1.refs_0_, bf16[3,512,256]{2,1,0:T(8,128)(2,1)S(1)} %select_convert_fusion.refs_1_, bf16[2,2,64,1024]{3,2,1,0:T(8,128)(2,1)S(1)} %copy-done.1, ...), custom_call_target="tpu_custom_call" | custom-call | flops 1073741824 | bytes 4194304 | tf_op jit(solution)/shard_map/pallas_call | solution.py:219
  23.1 0.0 collective-permute-done.2.refs_5_
  23.1 1.0 %shard_map.48.refs_7_ = bf16[2,64,1024]{2,1,0:T(8,128)(2,1)S(1)} custom-call(s32[6,2]{1,0:T(8,128)S(1)} %table.1.refs_0_, bf16[3,512,256]{2,1,0:T(8,128)(2,1)S(1)} %select_convert_fusion.refs_1_, bf16[2,2,64,1024]{3,2,1,0:T(8,128)(2,1)S(1)} %copy-done.1, bf16[2,2,2,1024]{3,2,1,0:T(2,128)(2,1)S(1)} %collective-permute-done.refs_3_.refs_5_.own_edge, ...), custom_call_target="tpu_custom_call" | custom-call | flops 1073741824 | bytes 4194304 | tf_op jit(solution)/shard_map/pallas_call | solution.py:219
  24.1 0.1 collective-permute-done.5.refs_5_.refs_4_
  24.3 1.2 %shard_map.49.refs_8_ = bf16[2,4,64,1024]{3,2,1,0:T(8,128)(2,1)} custom-call(s32[6,2]{1,0:T(8,128)S(1)} %table.1.refs_0_, bf16[3,512,256]{2,1,0:T(8,128)(2,1)S(1)} %select_convert_fusion.refs_1_, bf16[2,2,64,1024]{3,2,1,0:T(8,128)(2,1)S(1)} %copy-done.1, bf16[2,2,2,1024]{3,2,1,0:T(2,128)(2,1)S(1)} %collective-permute-done.refs_3_.refs_5_.own_edge, ...), custom_call_target="tpu_custom_call" | custom-call | flops 1073741824 | bytes 4194304 | tf_op jit(solution)/shard_map/pallas_call | solution.py:219
  25.5 5.3 %collective-permute-done.4.refs_4_ = bf16[1,128,1024]{2,1,0:T(8,128)(2,1)S(1)} collective-permute-done((bf16[1,128,1024]{2,1,0:T(8,128)(2,1)S(1)}, bf16[1,128,1024]{2,1,0:T(8,128)(2,1)S(1)}, u32[]{:S(2)}, u32[]{:S(2)}) %collective-permute-start.4) | collective-permute-done | bytes 262176 | tf_op jit(solution)/shard_map/ppermute | solution.py:333
  30.7 1.0 %shard_map.47.refs_7_ = bf16[2,64,1024]{2,1,0:T(8,128)(2,1)S(1)} custom-call(s32[6,2]{1,0:T(8,128)S(1)} %table.1.refs_0_, bf16[3,512,256]{2,1,0:T(8,128)(2,1)S(1)} %select_convert_fusion.refs_1_, bf16[2,2,64,1024]{3,2,1,0:T(8,128)(2,1)S(1)} %copy-done.1, bf16[2,2,2,1024]{3,2,1,0:T(2,128)(2,1)S(1)} %collective-permute-done.refs_3_.refs_5_.own_edge, ...), custom_call_target="tpu_custom_call" | custom-call | flops 1073741824 | bytes 4194304 | tf_op jit(solution)/shard_map/pallas_call | solution.py:219
  31.8 0.0 collective-permute-done.1.refs_4_
  31.8 1.7 %shard_map.50 = bf16[2,4,64,1024]{3,2,1,0:T(8,128)(2,1)} custom-call(s32[6,2]{1,0:T(8,128)S(1)} %table.1.refs_0_, bf16[3,512,256]{2,1,0:T(8,128)(2,1)S(1)} %select_convert_fusion.refs_1_, bf16[2,2,64,1024]{3,2,1,0:T(8,128)(2,1)S(1)} %copy-done.1, ...), custom_call_target="tpu_custom_call", output_to_operand_aliasing={{}: (8, {})} | custom-call | flops 1073741824 | bytes 4194304 | tf_op jit(solution)/shard_map/pallas_call | solution.py:219
  (10 shorter events, 0.1 us)
Async XLA Ops:
  0.0 1.0 %copy-start = (bf16[2,2,64,1024]{3,2,1,0:T(8,128)(2,1)S(1)}, bf16[2,2,64,1024]{3,2,1,0:T(8,128)(2,1)}, u32[]{:S(2)}) copy-start(bf16[2,2,64,1024]{3,2,1,0:T(8,128)(2,1)} %refs_2_.9) | copy-start | bytes 1572868
  1.0 9.1 %copy-start.1 = (bf16[2,2,64,1024]{3,2,1,0:T(8,128)(2,1)S(1)}, bf16[2,2,64,1024]{3,2,1,0:T(8,128)(2,1)}, u32[]{:S(2)}) copy-start(bf16[2,2,64,1024]{3,2,1,0:T(8,128)(2,1)} %refs_2_.9) | copy-start | bytes 1572868
  1.1 22.0 %collective-permute-start.2 = (bf16[2,2,2,1024]{3,2,1,0:T(2,128)(2,1)S(1)}, bf16[2,2,2,1024]{3,2,1,0:T(2,128)(2,1)S(1)}, u32[]{:S(2)}, u32[]{:S(2)}) collective-permute-start(bf16[2,2,2,1024]{3,2,1,0:T(2,128)(2,1)S(1)} %get-tuple-element.10), channel_id=1, source_target_pairs={{5,0},{4,1},{7,2},{6,3},{9,4},{8,5},{11,6},{10,7},{13,8},{12,9},{1... | collective-permute-start | bytes 49160 | tf_op jit(solution)/shard_map/ppermute | solution.py:361
  5.7 4.5 %collective-permute-start = (bf16[2,2,2,1024]{3,2,1,0:T(2,128)(2,1)S(1)}, bf16[2,2,2,1024]{3,2,1,0:T(2,128)(2,1)S(1)}, u32[]{:S(2)}, u32[]{:S(2)}) collective-permute-start(bf16[2,2,2,1024]{3,2,1,0:T(2,128)(2,1)S(1)} %get-tuple-element.10), channel_id=1, source_target_pairs={{1,0},{0,1},{3,2},{2,3},{5,4},{4,5},{7,6},{6,7},{9,8},{8,9},{11,10... | collective-permute-start | bytes 49160 | tf_op jit(solution)/shard_map/ppermute | solution.py:361
  6.3 25.5 %collective-permute-start.1 = (bf16[1,128,1024]{2,1,0:T(8,128)(2,1)S(1)}, bf16[1,128,1024]{2,1,0:T(8,128)(2,1)S(1)}, u32[]{:S(2)}, u32[]{:S(2)}) collective-permute-start(bf16[1,128,1024]{2,1,0:T(8,128)(2,1)S(1)} %get-tuple-element.11), channel_id=1, source_target_pairs={{4,0},{6,2},{8,4},{10,6},{12,8},{14,10},{0,12},{2,14},{5,1},{7,3},... | collective-permute-start | bytes 786440 | tf_op jit(solution)/shard_map/ppermute | solution.py:331
  6.8 14.3 %collective-permute-start.3 = (bf16[1,128,1024]{2,1,0:T(8,128)(2,1)S(1)}, bf16[1,128,1024]{2,1,0:T(8,128)(2,1)S(1)}, u32[]{:S(2)}, u32[]{:S(2)}) collective-permute-start(bf16[1,128,1024]{2,1,0:T(8,128)(2,1)S(1)} %get-tuple-element.13), channel_id=1, source_target_pairs={{4,0},{6,2},{8,4},{10,6},{12,8},{14,10},{0,12},{2,14},{5,1},{7,3},... | collective-permute-start | bytes 786440 | tf_op jit(solution)/shard_map/ppermute | solution.py:328
  7.5 0.7 %copy-start.2 = (s32[2,4]{1,0:T(2,128)S(1)}, s32[2,4]{1,0:T(2,128)}, u32[]{:S(2)}) copy-start(s32[2,4]{1,0:T(2,128)} %partners.1) | copy-start | bytes 100
  8.2 0.7 %copy-start.3 = (s32[2,4]{1,0:T(2,128)S(1)}, s32[2,4]{1,0:T(2,128)}, u32[]{:S(2)}) copy-start(s32[2,4]{1,0:T(2,128)} %windows.1) | copy-start | bytes 100
  8.9 0.7 %copy-start.4 = (s32[2]{0:T(128)S(1)}, s32[2]{0:T(128)}, u32[]{:S(2)}) copy-start(s32[2]{0:T(128)} %counts.1) | copy-start | bytes 28
  10.2 14.1 %collective-permute-start.5 = (bf16[1,136,1024]{2,1,0:T(8,128)(2,1)S(1)}, bf16[1,136,1024]{2,1,0:T(8,128)(2,1)S(1)}, u32[]{:S(2)}, u32[]{:S(2)}) collective-permute-start(bf16[1,136,1024]{2,1,0:T(8,128)(2,1)S(1)} %attach.1), channel_id=1, source_target_pairs={{2,0},{4,2},{6,4},{8,6},{10,8},{12,10},{14,12},{0,14},{3,1},{5,3},... | collective-permute-start | bytes 835592 | tf_op jit(solution)/shard_map/ppermute | solution.py:329
  21.2 9.6 %collective-permute-start.4 = (bf16[1,128,1024]{2,1,0:T(8,128)(2,1)S(1)}, bf16[1,128,1024]{2,1,0:T(8,128)(2,1)S(1)}, u32[]{:S(2)}, u32[]{:S(2)}) collective-permute-start(bf16[1,128,1024]{2,1,0:T(8,128)(2,1)S(1)} %broadcast_select_fusion), channel_id=1, source_target_pairs={{2,0},{0,2},{6,4},{4,6},{10,8},{8,10},{14,12},{12,14},{3,1},{1,3},... | collective-permute-start | bytes 786440 | tf_op jit(solution)/shard_map/ppermute | solution.py:333

commit v5 on v4

--- a/solution.py
+++ b/solution.py
@@ -79,9 +79,6 @@
             return *stripe_of(other[0], t, stripe), *stripe_of(other[1], t, stripe)
         found = []
         for (k, start, base), size in zip(layout(stripe), (rows, rows, HALO, HALO)):
-            if len(other[k].shape) == 4:
-                found.append(other[k][start, base, :, stripe * LANES : (stripe + 1) * LANES].astype(jnp.float32))
-                continue
             columns = slice((stripe - base) * LANES, (stripe - base + 1) * LANES)
             found.append(other[k][0, start : start + size, columns].astype(jnp.float32))
         return found
@@ -322,24 +319,31 @@
     within = [(i + 1 - 2 * (i % 2), i) for i in range(loop_size)]
     is_odd = lax.rem(lax.axis_index("date"), 2) == 1
     cols = own.shape[3]
-    edge, first, far_part = prepare(own, ((((0, 0, 0), (0, 1, 0)), cols), (((1, 0, 0), (1, 1, 0)), cols)))
+    edge, first_re, second = prepare(own, ((((0, 0, 0),), cols), (((1, 0, 0), (1, 1, 0)), cols)))
     own_edge = edge_move(edge, 0)
-    near_part = attach(own, own_edge, ((1, 0, 0), (1, 1, 0)))
-    far_first = lax.ppermute(first, "date", by_two)
-    near_second = lax.ppermute(near_part, "date", by_one)
-    far_edge = edge_move(edge, 2)
-    far_second = lax.ppermute(far_part, "date", by_two)
-    chosen = jnp.where(is_odd, first, far_first)
-    near_first = lax.ppermute(chosen, "date", within)
-
-    def whole_edges(date):
-        return lambda stripe: ((0, 0, 0), (0, rows, 0), (1, date, 0), (1, date, 1))
+    parts = first_re, attach(own, own_edge, ((0, 1, 0),))
+    far = [lax.ppermute(part, "date", by_two) for part in parts]
+    near_second = lax.ppermute(attach(own, own_edge, ((1, 0, 0), (1, 1, 0))), "date", by_one)
+    far_second = lax.ppermute(second, "date", by_two)
+    near = []
+    for k, part in enumerate(parts):
+        chosen = jnp.where(is_odd, part, far[k])
+        near.append(lax.ppermute(chosen, "date", within))
+
+    def of_first(stripe):
+        return (0, 0, 0), (1, 0, 0), (1, rows, 0), (1, rows + HALO, 0)
+
+    def of_near_second(stripe):
+        return (0, 0, 0), (0, rows, 0), (0, 2 * rows + 2 * HALO, 0), (0, 2 * rows + 3 * HALO, 0)
+
+    def of_far_second(stripe):
+        return (0, 0, 0), (0, rows, 0), (1, rows + 2 * HALO, 0), (1, rows + 3 * HALO, 0)
 
     return own_edge, [
-        ((4,), [far_first, far_edge], whole_edges(0), None),
-        ((3,), [near_second], lambda stripe: ((0, 0, 0), (0, rows, 0), (0, 2 * rows + 2 * HALO, 0), (0, 2 * rows + 3 * HALO, 0)), None),
-        ((2,), [near_first, near_second], lambda stripe: ((0, 0, 0), (0, rows, 0), (1, 2 * rows, 0), (1, 2 * rows + HALO, 0)), None),
-        ((5,), [far_second, far_edge], whole_edges(1), None),
+        ((4,), far, of_first, None),
+        ((3,), [near_second], of_near_second, None),
+        ((2,), near, of_first, None),
+        ((5,), [far_second, far[1]], of_far_second, None),
     ]
 
 

time: 33.7 us -> 29 us (0.86)
  waiting for transfers between devices: 14.9 us -> 8.86 us
  starting transfers between devices: 8.22 us -> 9.37 us
    ppermute x4 -> x6, waiting for transfers between devices: 14.9 us -> 8.85 us  [the longest x2 5.21 us: relayed(): far = [lax.ppermute(part, 'date', by_two) for part in parts]]
    ppermute x4 -> x6, starting transfers between devices: 2.98 us -> 8.81 us  [the longest x2 5.15 us: relayed(): far = [lax.ppermute(part, 'date', by_two) for part in parts]]
    ppermute x2 -> x1, starting transfers between devices: 5.25 us -> 0.56 us  [edge_move(): return lax.ppermute(edge, ('date', 'row'), pairs)]
  transfers between devices with their start and end apart: 6 -> 7, of which waited for: 3 -> 3; matrix products, arithmetic and copies ran while one was open for 1% -> 1% of each run, Pallas kernels for 16% -> 18%
where the time goes in v5:
time: 29 us; the launch traced here: 28.7 us
  starting transfers between devices  9.37 us (32%)
  waiting for transfers between devices  8.86 us (31%)
  Pallas kernels  7.03 us (24%)
  local copies, waits for them, and re-layouts  3.05 us (11%)
  other arithmetic  0.31 us (1%)
    pallas_call x5, Pallas kernels, stage(): pl.pallas_call(functools.partial(stage_kernel, role, rows_of, layout, spa...  6.32 us
    ppermute x2, waiting for transfers between devices, relayed(): far = [lax.ppermute(part, 'date', by_two) for part in parts]  5.21 us
    ppermute x2, starting transfers between devices, relayed(): far = [lax.ppermute(part, 'date', by_two) for part in parts]  5.15 us
    ppermute x1, waiting for transfers between devices, relayed(): lax.ppermute(attach(own, own_edge, ((1, 0, 0), (1, 1, 0))), 'date', by_one)  3.31 us
    unnamed x10, local copies, waits for them, and re-layouts  3.05 us
    ppermute x2, starting transfers between devices, relayed(): near.append(lax.ppermute(chosen, 'date', within))  1.75 us
    ppermute x1, starting transfers between devices, relayed(): lax.ppermute(attach(own, own_edge, ((1, 0, 0), (1, 1, 0))), 'date', by_one)  1.46 us
    pallas_call x1, Pallas kernels, table_of(): pl.pallas_call(functools.partial(table_kernel, total_dates, partners.shap...  0.62 us
  transfers between devices with their start and end apart: 7, of which 3 were waited for; matrix products, arithmetic and copies ran while one was open for 1% of the time, Pallas kernels for 18%

profile of v5, /device:TPU:0, one launch (start us, length us, event | category | flops | bytes accessed | tf_op | source)
XLA Modules:
  0.0 28.7 jit_solution(12546621124544204567)
XLA Ops:
  0.0 1.0 %copy-done = bf16[2,2,64,1024]{3,2,1,0:T(8,128)(2,1)S(1)} copy-done((bf16[2,2,64,1024]{3,2,1,0:T(8,128)(2,1)S(1)}, bf16[2,2,64,1024]{3,2,1,0:T(8,128)(2,1)}, u32[]{:S(2)}) %copy-start) | copy-done | bytes 524312
  1.1 0.6 %collective-permute-start = (bf16[2,2,2,1024]{3,2,1,0:T(2,128)(2,1)S(1)}, bf16[2,2,2,1024]{3,2,1,0:T(2,128)(2,1)S(1)}, u32[]{:S(2)}, u32[]{:S(2)}) collective-permute-start(bf16[2,2,2,1024]{3,2,1,0:T(2,128)(2,1)S(1)} %get-tuple-element.10), channel_id=1, source_target_pairs={{1,0},{0,1},{3,2},{2,3},{5,4},{4,5},{7,6},{6,7},{9,8},{8,9},{11,10... | collective-permute-start | bytes 49160 | tf_op jit(solution)/shard_map/ppermute | solution.py:365
  1.6 4.7 %collective-permute-start.3 = (bf16[1,64,1024]{2,1,0:T(8,128)(2,1)S(1)}, bf16[1,64,1024]{2,1,0:T(8,128)(2,1)S(1)}, u32[]{:S(2)}, u32[]{:S(2)}) collective-permute-start(bf16[1,64,1024]{2,1,0:T(8,128)(2,1)S(1)} %get-tuple-element.13), channel_id=1, source_target_pairs={{4,0},{6,2},{8,4},{10,6},{12,8},{14,10},{0,12},{2,14},{5,1},{7,3},... | collective-permute-start | bytes 393224 | tf_op jit(solution)/shard_map/ppermute | solution.py:325
  6.3 0.4 %collective-permute-start.1 = (bf16[1,128,1024]{2,1,0:T(8,128)(2,1)S(1)}, bf16[1,128,1024]{2,1,0:T(8,128)(2,1)S(1)}, u32[]{:S(2)}, u32[]{:S(2)}) collective-permute-start(bf16[1,128,1024]{2,1,0:T(8,128)(2,1)S(1)} %get-tuple-element.11), channel_id=1, source_target_pairs={{4,0},{6,2},{8,4},{10,6},{12,8},{14,10},{0,12},{2,14},{5,1},{7,3},... | collective-permute-start | bytes 786440 | tf_op jit(solution)/shard_map/ppermute | solution.py:327
  6.8 0.3 select_convert_fusion.refs_1_
  7.0 0.0 copy-start.2
  7.0 0.7 %copy-done.2 = s32[2,4]{1,0:T(2,128)S(1)} copy-done((s32[2,4]{1,0:T(2,128)S(1)}, s32[2,4]{1,0:T(2,128)}, u32[]{:S(2)}) %copy-start.2) | copy-done | bytes 56
  7.7 0.7 %copy-done.3 = s32[2,4]{1,0:T(2,128)S(1)} copy-done((s32[2,4]{1,0:T(2,128)S(1)}, s32[2,4]{1,0:T(2,128)}, u32[]{:S(2)}) %copy-start.3) | copy-done | bytes 56
  8.4 0.7 %copy-done.4 = s32[2]{0:T(128)S(1)} copy-done((s32[2]{0:T(128)S(1)}, s32[2]{0:T(128)}, u32[]{:S(2)}) %copy-start.4) | copy-done | bytes 32
  9.1 0.6 %table.1.refs_0_ = s32[6,2]{1,0:T(8,128)S(1)} custom-call(s32[2,4]{1,0:T(2,128)S(1)} %copy-done.2, s32[2]{0:T(128)S(1)} %copy-done.4, s32[2,4]{1,0:T(2,128)S(1)} %copy-done.3), custom_call_target="tpu_custom_call" | custom-call | tf_op jit(solution)/shard_map/table/pallas_call | solution.py:281
  9.7 0.0 collective-permute-done.own_edge.refs_3_.refs_5_
  9.7 0.5 %collective-permute-start.2 = (bf16[1,72,1024]{2,1,0:T(8,128)(2,1)S(1)}, bf16[1,72,1024]{2,1,0:T(8,128)(2,1)S(1)}, u32[]{:S(2)}, u32[]{:S(2)}) collective-permute-start(bf16[1,72,1024]{2,1,0:T(8,128)(2,1)S(1)} %attach.2), channel_id=1, source_target_pairs={{4,0},{6,2},{8,4},{10,6},{12,8},{14,10},{0,12},{2,14},{5,1},{7,3},... | collective-permute-start | bytes 442376 | tf_op jit(solution)/shard_map/ppermute | solution.py:325
  10.3 1.5 %collective-permute-start.6 = (bf16[1,136,1024]{2,1,0:T(8,128)(2,1)S(1)}, bf16[1,136,1024]{2,1,0:T(8,128)(2,1)S(1)}, u32[]{:S(2)}, u32[]{:S(2)}) collective-permute-start(bf16[1,136,1024]{2,1,0:T(8,128)(2,1)S(1)} %attach.3), channel_id=1, source_target_pairs={{2,0},{4,2},{6,4},{8,6},{10,8},{12,10},{14,12},{0,14},{3,1},{5,3},... | collective-permute-start | bytes 835592 | tf_op jit(solution)/shard_map/ppermute | solution.py:326
  11.7 1.3 %shard_map.46 = (bf16[4,64,1024]{2,1,0:T(8,128)(2,1)S(1)}, f32[2,3,64,1024]{3,2,1,0:T(8,128)S(1)}) custom-call(s32[6,2]{1,0:T(8,128)S(1)} %table.1.refs_0_, bf16[3,512,256]{2,1,0:T(8,128)(2,1)S(1)} %select_convert_fusion.refs_1_, bf16[2,2,64,1024]{3,2,1,0:T(8,128)(2,1)S(1)} %copy-done.1, ...), custom_call_target="tpu_custom_call" | custom-call | flops 1073741824 | bytes 4194304 | tf_op jit(solution)/shard_map/pallas_call | solution.py:216
  13.0 0.0 collective-permute-done.3.refs_4_
  13.1 0.7 %collective-permute-start.4 = (bf16[1,64,1024]{2,1,0:T(8,128)(2,1)S(1)}, bf16[1,64,1024]{2,1,0:T(8,128)(2,1)S(1)}, u32[]{:S(2)}, u32[]{:S(2)}) collective-permute-start(bf16[1,64,1024]{2,1,0:T(8,128)(2,1)S(1)} %broadcast_select_fusion.1), channel_id=1, source_target_pairs={{2,0},{0,2},{6,4},{4,6},{10,8},{8,10},{14,12},{12,14},{3,1},{1,3},... | collective-permute-start | bytes 393224 | tf_op jit(solution)/shard_map/ppermute | solution.py:331
  13.7 5.2 %collective-permute-done.2.refs_5_ = bf16[1,72,1024]{2,1,0:T(8,128)(2,1)S(1)} collective-permute-done((bf16[1,72,1024]{2,1,0:T(8,128)(2,1)S(1)}, bf16[1,72,1024]{2,1,0:T(8,128)(2,1)S(1)}, u32[]{:S(2)}, u32[]{:S(2)}) %collective-permute-start.2) | collective-permute-done | bytes 147488 | tf_op jit(solution)/shard_map/ppermute | solution.py:325
  19.0 1.1 %collective-permute-start.5 = (bf16[1,72,1024]{2,1,0:T(8,128)(2,1)S(1)}, bf16[1,72,1024]{2,1,0:T(8,128)(2,1)S(1)}, u32[]{:S(2)}, u32[]{:S(2)}) collective-permute-start(bf16[1,72,1024]{2,1,0:T(8,128)(2,1)S(1)} %broadcast_select_fusion), channel_id=1, source_target_pairs={{2,0},{0,2},{6,4},{4,6},{10,8},{8,10},{14,12},{12,14},{3,1},{1,3},... | collective-permute-start | bytes 442376 | tf_op jit(solution)/shard_map/ppermute | solution.py:331
  20.0 1.0 %shard_map.48.refs_7_ = bf16[2,64,1024]{2,1,0:T(8,128)(2,1)S(1)} custom-call(s32[6,2]{1,0:T(8,128)S(1)} %table.1.refs_0_, bf16[3,512,256]{2,1,0:T(8,128)(2,1)S(1)} %select_convert_fusion.refs_1_, bf16[2,2,64,1024]{3,2,1,0:T(8,128)(2,1)S(1)} %copy-done.1, bf16[2,2,2,1024]{3,2,1,0:T(2,128)(2,1)S(1)} %collective-permute-done.own_edge.refs_3_.refs_5_, ...), custom_call_target="tpu_custom_call" | custom-call | flops 1073741824 | bytes 4194304 | tf_op jit(solution)/shard_map/pallas_call | solution.py:216
  21.1 3.3 %collective-permute-done.6.refs_4_ = bf16[1,136,1024]{2,1,0:T(8,128)(2,1)S(1)} collective-permute-done((bf16[1,136,1024]{2,1,0:T(8,128)(2,1)S(1)}, bf16[1,136,1024]{2,1,0:T(8,128)(2,1)S(1)}, u32[]{:S(2)}, u32[]{:S(2)}) %collective-permute-start.6) | collective-permute-done | bytes 278560 | tf_op jit(solution)/shard_map/ppermute | solution.py:326
  24.4 1.2 %shard_map.49.refs_8_ = bf16[2,4,64,1024]{3,2,1,0:T(8,128)(2,1)} custom-call(s32[6,2]{1,0:T(8,128)S(1)} %table.1.refs_0_, bf16[3,512,256]{2,1,0:T(8,128)(2,1)S(1)} %select_convert_fusion.refs_1_, bf16[2,2,64,1024]{3,2,1,0:T(8,128)(2,1)S(1)} %copy-done.1, bf16[2,2,2,1024]{3,2,1,0:T(2,128)(2,1)S(1)} %collective-permute-done.own_edge.refs_3_.refs_5_, ...), custom_call_target="tpu_custom_call" | custom-call | flops 1073741824 | bytes 4194304 | tf_op jit(solution)/shard_map/pallas_call | solution.py:216
  25.6 0.3 %collective-permute-done.5.refs_5_ = bf16[1,72,1024]{2,1,0:T(8,128)(2,1)S(1)} collective-permute-done((bf16[1,72,1024]{2,1,0:T(8,128)(2,1)S(1)}, bf16[1,72,1024]{2,1,0:T(8,128)(2,1)S(1)}, u32[]{:S(2)}, u32[]{:S(2)}) %collective-permute-start.5) | collective-permute-done | bytes 147488 | tf_op jit(solution)/shard_map/ppermute | solution.py:331
  25.9 1.0 %shard_map.47.refs_7_ = bf16[2,64,1024]{2,1,0:T(8,128)(2,1)S(1)} custom-call(s32[6,2]{1,0:T(8,128)S(1)} %table.1.refs_0_, bf16[3,512,256]{2,1,0:T(8,128)(2,1)S(1)} %select_convert_fusion.refs_1_, bf16[2,2,64,1024]{3,2,1,0:T(8,128)(2,1)S(1)} %copy-done.1, bf16[2,2,2,1024]{3,2,1,0:T(2,128)(2,1)S(1)} %collective-permute-done.own_edge.refs_3_.refs_5_, ...), custom_call_target="tpu_custom_call" | custom-call | flops 1073741824 | bytes 4194304 | tf_op jit(solution)/shard_map/pallas_call | solution.py:216
  27.0 1.7 %shard_map.50 = bf16[2,4,64,1024]{3,2,1,0:T(8,128)(2,1)} custom-call(s32[6,2]{1,0:T(8,128)S(1)} %table.1.refs_0_, bf16[3,512,256]{2,1,0:T(8,128)(2,1)S(1)} %select_convert_fusion.refs_1_, bf16[2,2,64,1024]{3,2,1,0:T(8,128)(2,1)S(1)} %copy-done.1, ...), custom_call_target="tpu_custom_call", output_to_operand_aliasing={{}: (8, {})} | custom-call | flops 1073741824 | bytes 4194304 | tf_op jit(solution)/shard_map/pallas_call | solution.py:216
  (14 shorter events, 0.1 us)
Async XLA Ops:
  0.0 1.0 %copy-start = (bf16[2,2,64,1024]{3,2,1,0:T(8,128)(2,1)S(1)}, bf16[2,2,64,1024]{3,2,1,0:T(8,128)(2,1)}, u32[]{:S(2)}) copy-start(bf16[2,2,64,1024]{3,2,1,0:T(8,128)(2,1)} %refs_2_.9) | copy-start | bytes 1572868
  1.0 8.6 %copy-start.1 = (bf16[2,2,64,1024]{3,2,1,0:T(8,128)(2,1)S(1)}, bf16[2,2,64,1024]{3,2,1,0:T(8,128)(2,1)}, u32[]{:S(2)}) copy-start(bf16[2,2,64,1024]{3,2,1,0:T(8,128)(2,1)} %refs_2_.9) | copy-start | bytes 1572868
  1.1 8.6 %collective-permute-start = (bf16[2,2,2,1024]{3,2,1,0:T(2,128)(2,1)S(1)}, bf16[2,2,2,1024]{3,2,1,0:T(2,128)(2,1)S(1)}, u32[]{:S(2)}, u32[]{:S(2)}) collective-permute-start(bf16[2,2,2,1024]{3,2,1,0:T(2,128)(2,1)S(1)} %get-tuple-element.10), channel_id=1, source_target_pairs={{1,0},{0,1},{3,2},{2,3},{5,4},{4,5},{7,6},{6,7},{9,8},{8,9},{11,10... | collective-permute-start | bytes 49160 | tf_op jit(solution)/shard_map/ppermute | solution.py:365
  1.6 11.4 %collective-permute-start.3 = (bf16[1,64,1024]{2,1,0:T(8,128)(2,1)S(1)}, bf16[1,64,1024]{2,1,0:T(8,128)(2,1)S(1)}, u32[]{:S(2)}, u32[]{:S(2)}) collective-permute-start(bf16[1,64,1024]{2,1,0:T(8,128)(2,1)S(1)} %get-tuple-element.13), channel_id=1, source_target_pairs={{4,0},{6,2},{8,4},{10,6},{12,8},{14,10},{0,12},{2,14},{5,1},{7,3},... | collective-permute-start | bytes 393224 | tf_op jit(solution)/shard_map/ppermute | solution.py:325
  6.3 20.7 %collective-permute-start.1 = (bf16[1,128,1024]{2,1,0:T(8,128)(2,1)S(1)}, bf16[1,128,1024]{2,1,0:T(8,128)(2,1)S(1)}, u32[]{:S(2)}, u32[]{:S(2)}) collective-permute-start(bf16[1,128,1024]{2,1,0:T(8,128)(2,1)S(1)} %get-tuple-element.11), channel_id=1, source_target_pairs={{4,0},{6,2},{8,4},{10,6},{12,8},{14,10},{0,12},{2,14},{5,1},{7,3},... | collective-permute-start | bytes 786440 | tf_op jit(solution)/shard_map/ppermute | solution.py:327
  7.0 0.7 %copy-start.2 = (s32[2,4]{1,0:T(2,128)S(1)}, s32[2,4]{1,0:T(2,128)}, u32[]{:S(2)}) copy-start(s32[2,4]{1,0:T(2,128)} %partners.1) | copy-start | bytes 100
  7.7 0.7 %copy-start.3 = (s32[2,4]{1,0:T(2,128)S(1)}, s32[2,4]{1,0:T(2,128)}, u32[]{:S(2)}) copy-start(s32[2,4]{1,0:T(2,128)} %windows.1) | copy-start | bytes 100
  8.4 0.7 %copy-start.4 = (s32[2]{0:T(128)S(1)}, s32[2]{0:T(128)}, u32[]{:S(2)}) copy-start(s32[2]{0:T(128)} %counts.1) | copy-start | bytes 28
  9.7 9.2 %collective-permute-start.2 = (bf16[1,72,1024]{2,1,0:T(8,128)(2,1)S(1)}, bf16[1,72,1024]{2,1,0:T(8,128)(2,1)S(1)}, u32[]{:S(2)}, u32[]{:S(2)}) collective-permute-start(bf16[1,72,1024]{2,1,0:T(8,128)(2,1)S(1)} %attach.2), channel_id=1, source_target_pairs={{4,0},{6,2},{8,4},{10,6},{12,8},{14,10},{0,12},{2,14},{5,1},{7,3},... | collective-permute-start | bytes 442376 | tf_op jit(solution)/shard_map/ppermute | solution.py:325
  10.3 14.1 %collective-permute-start.6 = (bf16[1,136,1024]{2,1,0:T(8,128)(2,1)S(1)}, bf16[1,136,1024]{2,1,0:T(8,128)(2,1)S(1)}, u32[]{:S(2)}, u32[]{:S(2)}) collective-permute-start(bf16[1,136,1024]{2,1,0:T(8,128)(2,1)S(1)} %attach.3), channel_id=1, source_target_pairs={{2,0},{4,2},{6,4},{8,6},{10,8},{12,10},{14,12},{0,14},{3,1},{5,3},... | collective-permute-start | bytes 835592 | tf_op jit(solution)/shard_map/ppermute | solution.py:326
  13.1 12.5 %collective-permute-start.4 = (bf16[1,64,1024]{2,1,0:T(8,128)(2,1)S(1)}, bf16[1,64,1024]{2,1,0:T(8,128)(2,1)S(1)}, u32[]{:S(2)}, u32[]{:S(2)}) collective-permute-start(bf16[1,64,1024]{2,1,0:T(8,128)(2,1)S(1)} %broadcast_select_fusion.1), channel_id=1, source_target_pairs={{2,0},{0,2},{6,4},{4,6},{10,8},{8,10},{14,12},{12,14},{3,1},{1,3},... | collective-permute-start | bytes 393224 | tf_op jit(solution)/shard_map/ppermute | solution.py:331
  19.0 7.0 %collective-permute-start.5 = (bf16[1,72,1024]{2,1,0:T(8,128)(2,1)S(1)}, bf16[1,72,1024]{2,1,0:T(8,128)(2,1)S(1)}, u32[]{:S(2)}, u32[]{:S(2)}) collective-permute-start(bf16[1,72,1024]{2,1,0:T(8,128)(2,1)S(1)} %broadcast_select_fusion), channel_id=1, source_target_pairs={{2,0},{0,2},{6,4},{4,6},{10,8},{8,10},{14,12},{12,14},{3,1},{1,3},... | collective-permute-start | bytes 442376 | tf_op jit(solution)/shard_map/ppermute | solution.py:331
